TPU v7x, 32 devices: a whole 2x2x4 slice. The times are simulated.
32 devices in a mesh: grp: 2 (over x), long: 16 (over z, y, core).
Axes of the slice: x: 2, y: 2, z: 4, core: 2. Of those that a mesh axis runs over, the one named last changes fastest.
Arguments:
- pixel_map: int32 [256, 2048], P(('grp', 'long')), parts along dimension 0, may hold values from 0 to 3
- materials: float32 [8], P('grp'), parts along dimension 0, may hold values from 1.5 to 12
- mode_panel: float32 [128, 2, 201, 201], P(('grp', 'long')), parts along dimension 0, may hold values from -1.6 to 1.6
Outputs:
- coupled_panel: float32 [128, 2, 201, 201], P(('grp', 'long')), parts along dimension 0
There are 2 independent parts, one for each index of `grp`. A program takes and returns all parts, laid end to end along the dimension named above; each array names one. Nothing has to cross between parts.
All inputs are finite; a program needn't handle non-finite values.
Results may differ from a plain program's by a relative error of at most 0.0003.
Values sent between devices are 32-bit elements; how exact they have to be, the bound alone decides.
No kernel may reach another device: no remote copies, remote signals or barrier semaphores. Data moves between devices by JAX's collectives and lax.ppermute only.
A program may use at most 128 MiB of HBM per device.

v0:
```python
import functools
import math

import jax
import jax.numpy as jnp
import numpy as np
from jax import lax
from jax.experimental import pallas as pl
from jax.experimental.pallas import tpu as pltpu
from jax.sharding import PartitionSpec as P

NMAT = 4
NS_ITERS = 3
LANES = 128


def up(value, step):
    return -(-value // step) * step


def split(x):
    high = x.astype(jnp.bfloat16)
    low = (x - high.astype(jnp.float32)).astype(jnp.bfloat16)
    return high, low


def dot(a, b):
    return jnp.dot(a, b, preferred_element_type=jnp.float32)


def dot_split(a, b):
    return dot(a[0], b[0]) + dot(a[1], b[0]) + dot(a[0], b[1])


def split_table(table):
    table = np.asarray(table, np.float32)
    high = table.astype(jnp.bfloat16)
    low = (table - high.astype(np.float32)).astype(jnp.bfloat16)
    return np.stack([high, low])


def turn(product, period):
    return np.mod(product, period) * (2.0 * math.pi / period)


def pixel_tables(npix, order):
    width = up(order, LANES)
    k = np.arange(order)
    inner = np.zeros((LANES, 2 * width))
    angle = turn(np.arange(LANES)[:, None] * k[None, :], npix)
    inner[:, :order] = np.cos(angle) / npix
    inner[:, width : width + order] = np.sin(angle) / npix
    chunks = npix // LANES
    outer = np.zeros((chunks, 2 * width), np.float32)
    angle = turn(LANES * np.arange(chunks)[:, None] * k[None, :], npix)
    outer[:, :order] = np.cos(angle)
    outer[:, width : width + order] = np.sin(angle)
    return split_table(inner), outer


def symbol_table(order):
    width = up(order, LANES)
    k = np.arange(order)
    weight = np.where(k == 0, 1.0, 2.0)[:, None]
    table = np.zeros((2 * width, 2 * width))
    for half in range(2):
        angle = turn(k[:, None] * (2 * np.arange(order)[None, :] + half), 2 * order)
        columns = slice(half * width, half * width + order)
        table[:order, columns] = weight * np.cos(angle)
        table[width : width + order, columns] = weight * np.sin(angle)
    return split_table(table)


def order_tables(order, scale):
    width = up(order, LANES)
    centred = np.arange(order) - (order - 1) // 2
    whole = 2 * np.arange(order)
    angle = turn(centred[:, None] * whole[None, :], 2 * order)
    forward = np.zeros((width, 2 * width))
    forward[:order, :order] = np.cos(angle)
    forward[:order, width : width + order] = np.sin(angle)
    inverse = np.zeros((width, 2 * width))
    inverse[:order, :order] = np.cos(angle).T * (scale / order)
    inverse[:order, width : width + order] = np.sin(angle).T * (scale / order)
    gap = whole[:, None] - (whole + 1)[None, :]
    angle = turn(centred[:, None, None] * gap[None], 2 * order)
    step = np.zeros((width, width))
    step[:order, :order] = np.cos(angle).sum(0) / order
    return split_table(forward), split_table(inverse), split_table(step), split_table(step.T)


def line_tables(lines, yord, rows, kept):
    half = (yord - 1) // 2
    angle = turn(np.arange(lines)[:, None] * (np.arange(kept) - half)[None, :], lines)
    cosine, sine = np.zeros((lines, rows)), np.zeros((lines, rows))
    cosine[:, :kept], sine[:, :kept] = np.cos(angle), np.sin(angle)
    spread = np.block([[cosine, -sine], [sine, cosine]])
    return split_table(spread), split_table(spread.T)


def scale_of(materials):
    low = functools.reduce(jnp.minimum, materials)
    high = functools.reduce(jnp.maximum, materials)
    full = lambda value: jnp.full((1, LANES), value, jnp.float32)
    return 2.0 / (1.0 / full(low) + 1.0 / full(high))


def symbol_kernel(mats, pixels, inner, outer, table, out):
    materials = [mats[i] for i in range(NMAT)]
    inverse = [1.0 / jnp.full((1, LANES), m, jnp.float32) for m in materials]
    lines, npix = pixels.shape
    width = outer.shape[1] // 2
    chunks = npix // LANES
    parts = []
    for chunk in range(chunks):
        index = pixels[:, chunk * LANES : (chunk + 1) * LANES]
        value = jnp.zeros((lines, LANES), jnp.float32)
        for i in range(NMAT):
            value = value + jnp.where(index == i, inverse[i], 0.0)
        parts.append(value)
    inside = dot_split(split(jnp.concatenate(parts, 0)), (inner[0], inner[1]))
    real = jnp.zeros((lines, width), jnp.float32)
    imag = jnp.zeros((lines, width), jnp.float32)
    for chunk in range(chunks):
        rows = slice(chunk * lines, (chunk + 1) * lines)
        in_cos, in_sin = inside[rows, :width], inside[rows, width:]
        out_cos, out_sin = outer[chunk : chunk + 1, :width], outer[chunk : chunk + 1, width:]
        real = real + in_cos * out_cos - in_sin * out_sin
        imag = imag - in_cos * out_sin - in_sin * out_cos
    symbol = dot_split(split(jnp.concatenate([real, imag], 1)), (table[0], table[1]))
    out[...] = 0.5 - (0.5 * scale_of(materials)[0, 0]) * symbol


def panel_kernel(mats, symbol, panel, forward, inverse, step, back, to_lines, to_orders, out, folded, start, state):
    columns, _, yord, order = panel.shape
    rows = folded.shape[1] // 2
    lines = symbol.shape[0]
    kept = min(lines, yord)
    width = folded.shape[2]
    pair = lambda ref: (ref[0], ref[1])

    for c in range(columns):
        folded[c] = jnp.zeros((2 * rows, width), jnp.float32)
        for part in range(2):
            base = part * rows
            folded[c, base : base + kept, :order] = panel[c, part, :kept, :]
            for first in range(lines, yord, lines):
                count = min(lines, yord - first)
                folded[c, base : base + count, :order] += panel[c, part, first : first + count, :]
        both = dot_split(split(folded[c]), pair(forward))
        cosine, sine = both[:, :width], both[:, width:]
        real = cosine[:rows] + sine[rows:]
        imag = cosine[rows:] - sine[:rows]
        high, low = split(jnp.concatenate([real, imag], 0))
        value = dot(to_lines[0], high) + dot(to_lines[1], high) + dot(to_lines[0], low)
        start[c] = value
        state[c] = value

    def sweep(_, carry):
        whole = symbol[:, :width]
        half = symbol[:, width:]
        for c in range(columns):
            now = state[c]
            other = dot_split(split(now), pair(step))
            other = jnp.concatenate([other[:lines] * half, other[lines:] * half], 0)
            same = jnp.concatenate([now[:lines] * whole, now[lines:] * whole], 0)
            state[c] = start[c] + same + dot_split(split(other), pair(back))
        return carry

    lax.fori_loop(0, 2**NS_ITERS - 1, sweep, 0)

    factor = scale_of([mats[i] for i in range(NMAT)])[0, 0]
    for c in range(columns):
        high, low = split(state[c])
        value = dot(to_orders[0], high) + dot(to_orders[1], high) + dot(to_orders[0], low)
        both = dot_split(split(value * factor), pair(inverse))
        cosine, sine = both[:, :width], both[:, width:]
        real = cosine[:rows] - sine[rows:]
        imag = cosine[rows:] + sine[:rows]
        for part, value in enumerate((real, imag)):
            for first in range(0, yord, lines):
                count = min(lines, yord - first)
                out[c, part, first : first + count, :] = value[:count, :order]


SMEM = pl.BlockSpec(memory_space=pltpu.SMEM)
VMEM = pl.BlockSpec(memory_space=pltpu.VMEM)


def local(pixel_map, materials, mode_panel):
    devices = lax.axis_size("long")
    own, npix = pixel_map.shape
    lines = own * devices
    columns, _, yord, order = mode_panel.shape
    width = up(order, LANES)
    kept = min(lines, yord)
    rows = up(kept, 16)

    inner, outer = pixel_tables(npix, order)
    mine = pl.pallas_call(
        symbol_kernel,
        out_shape=jax.ShapeDtypeStruct((own, 2 * width), jnp.float32),
        in_specs=[SMEM] + [VMEM] * 4,
        out_specs=VMEM,
        name="symbol",
    )(materials, pixel_map, inner, outer, symbol_table(order))
    everyone = jnp.broadcast_to(mine[None], (devices,) + mine.shape)
    symbol = lax.all_to_all(everyone, "long", split_axis=0, concat_axis=0).reshape(lines, 2 * width)

    forward, inverse, step, back = order_tables(order, 1.0 / lines)
    to_lines, to_orders = line_tables(lines, yord, rows, kept)
    return pl.pallas_call(
        panel_kernel,
        out_shape=jax.ShapeDtypeStruct(mode_panel.shape, jnp.float32),
        in_specs=[SMEM] + [VMEM] * 8,
        out_specs=VMEM,
        scratch_shapes=[
            pltpu.VMEM((columns, 2 * rows, width), jnp.float32),
            pltpu.VMEM((columns, 2 * lines, width), jnp.float32),
            pltpu.VMEM((columns, 2 * lines, width), jnp.float32),
        ],
        compiler_params=pltpu.CompilerParams(vmem_limit_bytes=48 * 2**20),
        name="panel",
    )(materials, symbol, mode_panel, forward, inverse, step, back, to_lines, to_orders)


def solution(mesh):
    in_specs = (P(("grp", "long"), None), P("grp"), P(("grp", "long"), None, None, None))
    out_specs = P(("grp", "long"), None, None, None)
    return jax.shard_map(local, mesh=mesh, in_specs=in_specs, out_specs=out_specs, check_vma=False)
```

profile of v0, /device:TPU:0, one launch (start us, length us, event | category | flops | bytes accessed | tf_op | source)
XLA Modules:
  0.0 39.7 jit_solution(4275573412437895172)
XLA Ops:
  0.0 2.5 %symbol.1 = f32[8,512]{1,0:T(8,128)} custom-call(f32[4]{0:T(128)} %mats.3, s32[8,2048]{1,0:T(8,128)} %pixels.1, bf16[2,128,512]{2,1,0:T(8,128)(2,1)} %constant.18.clone.inner, f32[16,512]{1,0:T(8,128)} %constant.19.clone.outer, bf16[2,512,512]{2,1,0:T(8,128)(2,1)} %constant.20.clone.table), custom_call_target="tpu_custom_call" | custom-call | tf_op jit(solution)/shard_map/symbol/pallas_call | solution.py:200
  2.5 1.4 %broadcast_in_dim.2 = f32[16,8,512]{2,1,0:T(8,128)} broadcast(f32[8,512]{1,0:T(8,128)} %symbol.1), dimensions={1,2} | broadcast | bytes 278528 | tf_op jit(solution)/shard_map/broadcast_in_dim | solution.py:207
  4.0 7.4 %all-to-all-start = ((f32[16,8,512]{2,1,0:T(8,128)}), f32[16,8,512]{2,1,0:T(8,128)S(1)}, u32[]{:S(2)}, u32[]{:S(2)}) async-start(f32[16,8,512]{2,1,0:T(8,128)} %broadcast_in_dim.2), calls=%async_computation | async-start | bytes 524288 | tf_op jit(solution)/shard_map/all_to_all | solution.py:208
  11.4 0.0 copy-start
  11.4 0.0 copy-start.1
  11.4 0.0 copy-start.2
  11.4 0.0 copy-start.3
  11.4 0.0 copy-start.6
  11.5 1.7 %copy.13.panel = f32[4,2,201,201]{3,2,1,0:T(8,128)S(1)} copy(f32[4,2,201,201]{3,1,2,0:T(2,128)} %param.14) | data formatting | bytes 2585664 | tf_op args[2]
  13.2 8.2 %all-to-all-done = f32[16,8,512]{2,1,0:T(8,128)S(1)} async-done(((f32[16,8,512]{2,1,0:T(8,128)}), f32[16,8,512]{2,1,0:T(8,128)S(1)}, u32[]{:S(2)}, u32[]{:S(2)}) %all-to-all-start) | async-done | bytes 262176 | tf_op jit(solution)/shard_map/all_to_all | solution.py:208
  21.4 0.0 copy-done
  21.4 0.0 copy-done.1
  21.4 0.0 copy-done.2
  21.4 0.0 copy-done.3
  21.4 0.0 copy-done.6
  21.4 0.0 copy-start.4
  21.4 0.9 %copy-done.4 = bf16[2,256,256]{2,1,0:T(8,128)(2,1)S(1)} copy-done((bf16[2,256,256]{2,1,0:T(8,128)(2,1)S(1)}, bf16[2,256,256]{2,1,0:T(8,128)(2,1)}, u32[]{:S(2)}) %copy-start.4) | copy-done | bytes 262168
  22.4 0.0 copy-start.5
  22.4 0.9 %copy-done.5 = bf16[2,256,256]{2,1,0:T(8,128)(2,1)S(1)} copy-done((bf16[2,256,256]{2,1,0:T(8,128)(2,1)S(1)}, bf16[2,256,256]{2,1,0:T(8,128)(2,1)}, u32[]{:S(2)}) %copy-start.5) | copy-done | bytes 262168
  23.3 13.9 %panel.2 = f32[4,2,201,201]{3,2,1,0:T(8,128)S(1)} custom-call(f32[4]{0:T(128)S(1)} %copy-done.6, f32[128,512]{1,0:T(8,128)S(1)} %bitcast.1, f32[4,2,201,201]{3,2,1,0:T(8,128)S(1)} %copy.13.panel, bf16[2,256,512]{2,1,0:T(8,128)(2,1)S(1)} %copy-done.1, bf16[2,256,512]{2,1,0:T(8,128)(2,1)S(1)} %copy-done, bf16[2,256,256]{2,1,0:T(8,128)(2,1)S(1)} %copy-done.5, ...), custom_call_target="tpu_custom_call" | custom-call | tf_op jit(solution)/shard_map/panel/pallas_call | solution.py:212
  37.2 2.4 %copy.14 = f32[4,2,201,201]{3,1,2,0:T(2,128)} copy(f32[4,2,201,201]{3,2,1,0:T(8,128)S(1)} %panel.2) | data formatting | bytes 2585664 | tf_op jit(solution)/shard_map/panel/pallas_call | solution.py:212
Async XLA Ops:
  4.0 17.4 %all-to-all-start = ((f32[16,8,512]{2,1,0:T(8,128)}), f32[16,8,512]{2,1,0:T(8,128)S(1)}, u32[]{:S(2)}, u32[]{:S(2)}) async-start(f32[16,8,512]{2,1,0:T(8,128)} %broadcast_in_dim.2), calls=%async_computation | async-start | bytes 524288 | tf_op jit(solution)/shard_map/all_to_all | solution.py:208
  11.4 10.0 %copy-start = (bf16[2,256,512]{2,1,0:T(8,128)(2,1)S(1)}, bf16[2,256,512]{2,1,0:T(8,128)(2,1)}, u32[]{:S(2)}) copy-start(bf16[2,256,512]{2,1,0:T(8,128)(2,1)} %constant.22.clone.inverse) | copy-start | bytes 1572868
  11.4 10.0 %copy-start.1 = (bf16[2,256,512]{2,1,0:T(8,128)(2,1)S(1)}, bf16[2,256,512]{2,1,0:T(8,128)(2,1)}, u32[]{:S(2)}) copy-start(bf16[2,256,512]{2,1,0:T(8,128)(2,1)} %constant.21.clone.forward) | copy-start | bytes 1572868
  11.4 10.0 %copy-start.2 = (bf16[2,256,256]{2,1,0:T(8,128)(2,1)S(1)}, bf16[2,256,256]{2,1,0:T(8,128)(2,1)}, u32[]{:S(2)}) copy-start(bf16[2,256,256]{2,1,0:T(8,128)(2,1)} %constant.26.clone.to_orders) | copy-start | bytes 786436
  11.4 10.0 %copy-start.3 = (bf16[2,256,256]{2,1,0:T(8,128)(2,1)S(1)}, bf16[2,256,256]{2,1,0:T(8,128)(2,1)}, u32[]{:S(2)}) copy-start(bf16[2,256,256]{2,1,0:T(8,128)(2,1)} %constant.25.clone.to_lines) | copy-start | bytes 786436
  11.4 10.0 %copy-start.6 = (f32[4]{0:T(128)S(1)}, f32[4]{0:T(128)}, u32[]{:S(2)}) copy-start(f32[4]{0:T(128)} %mats.3) | copy-start | bytes 52
  21.4 1.0 %copy-start.4 = (bf16[2,256,256]{2,1,0:T(8,128)(2,1)S(1)}, bf16[2,256,256]{2,1,0:T(8,128)(2,1)}, u32[]{:S(2)}) copy-start(bf16[2,256,256]{2,1,0:T(8,128)(2,1)} %constant.24.clone.back) | copy-start | bytes 786436
  22.4 0.9 %copy-start.5 = (bf16[2,256,256]{2,1,0:T(8,128)(2,1)S(1)}, bf16[2,256,256]{2,1,0:T(8,128)(2,1)}, u32[]{:S(2)}) copy-start(bf16[2,256,256]{2,1,0:T(8,128)(2,1)} %constant.23.clone.step) | copy-start | bytes 786436
where the time goes:
time: 40 us; the launch traced here: 39.7 us
  Pallas kernels  16.4 us (41%)
  waiting for transfers between devices  8.23 us (21%)
  local copies, waits for them, and re-layouts  7.52 us (19%)
  starting transfers between devices  7.41 us (19%)
    pallas_call x1, Pallas kernels, local(): pl.pallas_call(panel_kernel, out_shape=jax.ShapeDtypeStruct(mode_panel.sh...  13.9 us
    all_to_all x1, waiting for transfers between devices, local(): lax.all_to_all(everyone, 'long', split_axis=0, concat_axis=0)  8.23 us
    all_to_all x1, starting transfers between devices, local(): lax.all_to_all(everyone, 'long', split_axis=0, concat_axis=0)  7.41 us
    unnamed x15, local copies, waits for them, and re-layouts  3.64 us
    pallas_call x1, Pallas kernels, local(): pl.pallas_call(symbol_kernel, out_shape=jax.ShapeDtypeStruct((own, 2 * wi...  2.52 us
    pallas_call x1, local copies, waits for them, and re-layouts, local(): pl.pallas_call(panel_kernel, out_shape=jax.ShapeDtypeStruct(mode_panel.sh...  2.44 us
    broadcast_in_dim x1, local copies, waits for them, and re-layouts, local(): everyone = jnp.broadcast_to(mine[None], (devices,) + mine.shape)  1.44 us
  transfers between devices with their start and end apart: 1, of which 1 were waited for; matrix products, arithmetic and copies ran while one was open for 4% of the time, Pallas kernels for 0%

commit v1 on v0

--- a/solution.py
+++ b/solution.py
@@ -12,6 +12,7 @@
 NMAT = 4
 NS_ITERS = 3
 LANES = 128
+BLOCK = 128
 
 
 def up(value, step):
@@ -105,9 +106,8 @@
     return 2.0 / (1.0 / full(low) + 1.0 / full(high))
 
 
-def symbol_kernel(mats, pixels, inner, outer, table, out):
-    materials = [mats[i] for i in range(NMAT)]
-    inverse = [1.0 / jnp.full((1, LANES), m, jnp.float32) for m in materials]
+def coefficient_kernel(mats, pixels, inner, outer, out):
+    inverse = [1.0 / jnp.full((1, LANES), mats[i], jnp.float32) for i in range(NMAT)]
     lines, npix = pixels.shape
     width = outer.shape[1] // 2
     chunks = npix // LANES
@@ -127,60 +127,176 @@
         out_cos, out_sin = outer[chunk : chunk + 1, :width], outer[chunk : chunk + 1, width:]
         real = real + in_cos * out_cos - in_sin * out_sin
         imag = imag - in_cos * out_sin - in_sin * out_cos
-    symbol = dot_split(split(jnp.concatenate([real, imag], 1)), (table[0], table[1]))
-    out[...] = 0.5 - (0.5 * scale_of(materials)[0, 0]) * symbol
-
-
-def panel_kernel(mats, symbol, panel, forward, inverse, step, back, to_lines, to_orders, out, folded, start, state):
-    columns, _, yord, order = panel.shape
+    out[:, :width] = real
+    out[:, width:] = imag
+
+
+def pair(ref):
+    return ref[0], ref[1]
+
+
+def spread_kernel(panel, forward, to_lines, out, folded):
+    _, yord, _, order = panel.shape
+    width = out.shape[1]
     rows = folded.shape[1] // 2
-    lines = symbol.shape[0]
+    double_lines = to_lines.shape[1]
+    lines = double_lines // 2
     kept = min(lines, yord)
-    width = folded.shape[2]
-    pair = lambda ref: (ref[0], ref[1])
-
-    for c in range(columns):
+    for c in range(folded.shape[0]):
         folded[c] = jnp.zeros((2 * rows, width), jnp.float32)
         for part in range(2):
             base = part * rows
-            folded[c, base : base + kept, :order] = panel[c, part, :kept, :]
+            folded[c, base : base + kept, :order] = panel[c, :kept, part, :]
             for first in range(lines, yord, lines):
                 count = min(lines, yord - first)
-                folded[c, base : base + count, :order] += panel[c, part, first : first + count, :]
+                folded[c, base : base + count, :order] += panel[c, first : first + count, part, :]
         both = dot_split(split(folded[c]), pair(forward))
         cosine, sine = both[:, :width], both[:, width:]
         real = cosine[:rows] + sine[rows:]
         imag = cosine[rows:] - sine[:rows]
         high, low = split(jnp.concatenate([real, imag], 0))
         value = dot(to_lines[0], high) + dot(to_lines[1], high) + dot(to_lines[0], low)
-        start[c] = value
-        state[c] = value
-
-    def sweep(_, carry):
-        whole = symbol[:, :width]
-        half = symbol[:, width:]
+        out[c * double_lines : (c + 1) * double_lines, :] = value
+
+
+def sweeps(count, half, start_of, symbol, steps, state, now, other, sums):
+    lines, width = symbol.shape[0], state.shape[1]
+    blocks = half // BLOCK
+    per_section = blocks // 2
+
+    def rows(unit, block):
+        return slice(unit * half + block * BLOCK, unit * half + (block + 1) * BLOCK)
+
+    def symbol_rows(unit, block, part):
+        first = (unit * half + block * BLOCK) % lines
+        return symbol[first : first + BLOCK, part * width : (part + 1) * width]
+
+    def issue(stage, section):
+        high, low = now if stage == 0 else other
+        own = range(section * per_section, (section + 1) * per_section)
+        for unit in range(2):
+            for part in range(2):
+                pltpu.matmul_push_rhs(steps[2 * stage + part], part, unit)
+        for block in own:
+            for unit in range(2):
+                load = 0 if block == own[0] else None
+                pltpu.matmul_acc_lhs(sums[unit * blocks + block], high[rows(unit, block)], load_staged_rhs=load)
+                pltpu.matmul_acc_lhs(sums[unit * blocks + block], low[rows(unit, block)])
+        for block in own:
+            for unit in range(2):
+                load = 1 if block == own[0] else None
+                pltpu.matmul_acc_lhs(sums[unit * blocks + block], high[rows(unit, block)], load_staged_rhs=load)
+
+    def finish(stage, section):
+        for block in range(section * per_section, (section + 1) * per_section):
+            for unit in range(2):
+                place = rows(unit, block)
+                value = pltpu.matmul_pop(sums[unit * blocks + block])
+                if stage == 0:
+                    high, low = split(value * symbol_rows(unit, block, 1))
+                    other[0][place], other[1][place] = high, low
+                else:
+                    value = start_of(unit, block) + state[place] * symbol_rows(unit, block, 0) + value
+                    state[place] = value
+                    now[0][place], now[1][place] = split(value)
+
+    def sweep(last):
+        order = ((0, 0), (0, 1), (1, 0), (1, 1))
+        for index, unit in enumerate(order):
+            if index + 1 < len(order):
+                issue(*order[index + 1])
+            elif not last:
+                issue(*order[0])
+            finish(*unit)
+
+    issue(0, 0)
+    lax.fori_loop(0, count - 1, lambda _, carry: (sweep(False), carry)[1], 0)
+    sweep(True)
+
+
+def unit_product(lhs, rhs, unit, sums):
+    depth = lhs[0].shape[1]
+    tile = sums.shape[1]
+    for first in range(0, depth, tile):
+        inner = slice(first, first + tile)
+        for part in range(2):
+            pltpu.matmul_push_rhs(rhs[part][inner], part, unit)
+        pltpu.matmul_acc_lhs(sums, lhs[0][:, inner], load_staged_rhs=0)
+        pltpu.matmul_acc_lhs(sums, lhs[1][:, inner])
+        pltpu.matmul_acc_lhs(sums, lhs[0][:, inner], load_staged_rhs=1)
+    return pltpu.matmul_pop(sums)
+
+
+def apply_kernel(groups, owners, mats, me, *refs):
+    starts, refs = refs[:groups], refs[groups:]
+    pieces, refs = refs[: len(owners)], refs[len(owners) :]
+    table, steps, inverse, to_orders, out, coefficients, symbol, state, result, ready, *splits = refs
+    now, other = splits[:2], splits[2:]
+    columns, yord, _, order = out.shape
+    lines = coefficients.shape[0]
+    width = state.shape[1]
+    rows = to_orders.shape[1] // 2
+    half = state.shape[0] // 2
+    factor = scale_of([mats[i] for i in range(NMAT)])[0, 0]
+
+    for piece, ids in zip(pieces, owners):
+        own = piece.shape[0] // len(ids)
+        for index, distance in enumerate(ids):
+            place = pl.multiple_of((me[0] ^ distance) * own, own)
+            coefficients[pl.ds(place, own), :] = piece[index * own : (index + 1) * own]
+    values = split(coefficients[...])
+
+    def all_symbols(*sums):
+        for unit in range(2):
+            columns_of = slice(unit * width, (unit + 1) * width)
+            value = unit_product(values, (table.at[0, :, columns_of], table.at[1, :, columns_of]), unit, sums[unit])
+            symbol[:, columns_of] = 0.5 - (0.5 * factor) * value
+
+    pl.run_scoped(all_symbols, *[pltpu.ACC(unit)((lines, width), jnp.float32) for unit in range(2)])
+
+    share = state.shape[0] // groups
+    for group in range(groups):
+        place = slice(group * share, (group + 1) * share)
+        value = starts[group][...]
+        state[place] = value
+        now[0][place], now[1][place] = split(value)
+
+    def start_of(unit, block):
+        first = unit * half + block * BLOCK
+        return starts[first // share][first % share : first % share + BLOCK]
+
+    def run(*sums):
+        sweeps(2**NS_ITERS - 1, half, start_of, symbol, steps, state, now, other, sums)
+
+    pl.run_scoped(run, *[pltpu.ACC(unit)((BLOCK, width), jnp.float32) for unit in range(2) for _ in range(half // BLOCK)])
+
+    def finish(*sums):
         for c in range(columns):
-            now = state[c]
-            other = dot_split(split(now), pair(step))
-            other = jnp.concatenate([other[:lines] * half, other[lines:] * half], 0)
-            same = jnp.concatenate([now[:lines] * whole, now[lines:] * whole], 0)
-            state[c] = start[c] + same + dot_split(split(other), pair(back))
-        return carry
-
-    lax.fori_loop(0, 2**NS_ITERS - 1, sweep, 0)
-
-    factor = scale_of([mats[i] for i in range(NMAT)])[0, 0]
-    for c in range(columns):
-        high, low = split(state[c])
-        value = dot(to_orders[0], high) + dot(to_orders[1], high) + dot(to_orders[0], low)
-        both = dot_split(split(value * factor), pair(inverse))
-        cosine, sine = both[:, :width], both[:, width:]
-        real = cosine[:rows] - sine[rows:]
-        imag = cosine[rows:] + sine[:rows]
-        for part, value in enumerate((real, imag)):
-            for first in range(0, yord, lines):
-                count = min(lines, yord - first)
-                out[c, part, first : first + count, :] = value[:count, :order]
+            place = slice(c * 2 * lines, (c + 1) * 2 * lines)
+            data = now[0].at[place], now[1].at[place]
+            value = unit_product((to_orders[0], to_orders[1]), data, c % 2, sums[c % 2])
+            value = split(value * factor)
+            cosine, sine = (
+                unit_product(
+                    value,
+                    tuple(inverse.at[part, :, unit * width : (unit + 1) * width] for part in range(2)),
+                    unit,
+                    sums[2 + 2 * (c % buffers) + unit],
+                )
+                for unit in range(2)
+            )
+            real = cosine[:rows] - sine[rows:]
+            imag = cosine[rows:] + sine[:rows]
+            for part, value in enumerate((real, imag)):
+                for first in range(0, yord, lines):
+                    count = min(lines, yord - first)
+                    result[c, first : first + count, part, :] = value[:count, :order]
+            pltpu.make_async_copy(result.at[c], out.at[c], ready.at[c]).start()
+        for c in range(columns):
+            pltpu.make_async_copy(result.at[c], out.at[c], ready.at[c]).wait()
+
+    buffers = min(2, columns)
+    pl.run_scoped(finish, *[pltpu.ACC(i % 2)((2 * rows, width), jnp.float32) for i in range(2 + 2 * buffers)])
 
 
 SMEM = pl.BlockSpec(memory_space=pltpu.SMEM)
@@ -195,33 +311,76 @@
     width = up(order, LANES)
     kept = min(lines, yord)
     rows = up(kept, 16)
+    groups = 2 if columns % 2 == 0 else 1
+    share = columns // groups
+    total = columns * 2 * lines
+    limit = pltpu.CompilerParams(vmem_limit_bytes=24 * 2**20)
 
     inner, outer = pixel_tables(npix, order)
     mine = pl.pallas_call(
-        symbol_kernel,
+        coefficient_kernel,
         out_shape=jax.ShapeDtypeStruct((own, 2 * width), jnp.float32),
-        in_specs=[SMEM] + [VMEM] * 4,
+        in_specs=[SMEM] + [VMEM] * 3,
         out_specs=VMEM,
-        name="symbol",
-    )(materials, pixel_map, inner, outer, symbol_table(order))
-    everyone = jnp.broadcast_to(mine[None], (devices,) + mine.shape)
-    symbol = lax.all_to_all(everyone, "long", split_axis=0, concat_axis=0).reshape(lines, 2 * width)
+        cost_estimate=pl.CostEstimate(flops=3 * 10**9, bytes_accessed=2**22, transcendentals=0),
+        name="coefficient",
+    )(materials, pixel_map, inner, outer)
 
     forward, inverse, step, back = order_tables(order, 1.0 / lines)
     to_lines, to_orders = line_tables(lines, yord, rows, kept)
-    return pl.pallas_call(
-        panel_kernel,
-        out_shape=jax.ShapeDtypeStruct(mode_panel.shape, jnp.float32),
-        in_specs=[SMEM] + [VMEM] * 8,
-        out_specs=VMEM,
+
+    pieces, owners, starts = [mine], [(0,)], []
+    by_order = jnp.swapaxes(mode_panel, 1, 2)
+    distance = devices // 2
+    while distance:
+        held = jnp.concatenate(pieces, 0) if len(pieces) > 1 else mine
+        other = lax.ppermute(held, "long", [(i, i ^ distance) for i in range(devices)])
+        if len(starts) < groups:
+            group = len(starts)
+            start = pl.pallas_call(
+                spread_kernel,
+                grid=(1,),
+                out_shape=jax.ShapeDtypeStruct((share * 2 * lines, width), jnp.float32),
+                in_specs=[pl.BlockSpec((share, yord, 2, order), lambda _, group=group: (group, 0, 0, 0)), VMEM, VMEM],
+                out_specs=VMEM,
+                scratch_shapes=[pltpu.VMEM((share, 2 * rows, width), jnp.float32)],
+                compiler_params=limit,
+                cost_estimate=pl.CostEstimate(flops=10**9, bytes_accessed=2**21, transcendentals=0),
+                name="spread",
+            )(by_order, forward, to_lines)
+            start, other = lax.optimization_barrier((start, other))
+            starts.append(start)
+        owners.append(tuple(d ^ distance for ids in owners for d in ids))
+        pieces.append(other)
+        distance //= 2
+
+    half = [pltpu.VMEM((total, width), jnp.bfloat16)]
+    result = pl.pallas_call(
+        functools.partial(apply_kernel, groups, owners),
+        out_shape=jax.ShapeDtypeStruct(by_order.shape, jnp.float32),
+        in_specs=[SMEM, SMEM] + [VMEM] * (4 + groups + len(pieces)),
+        out_specs=pl.BlockSpec(memory_space=pl.ANY),
         scratch_shapes=[
-            pltpu.VMEM((columns, 2 * rows, width), jnp.float32),
-            pltpu.VMEM((columns, 2 * lines, width), jnp.float32),
-            pltpu.VMEM((columns, 2 * lines, width), jnp.float32),
-        ],
-        compiler_params=pltpu.CompilerParams(vmem_limit_bytes=48 * 2**20),
-        name="panel",
-    )(materials, symbol, mode_panel, forward, inverse, step, back, to_lines, to_orders)
+            pltpu.VMEM((lines, 2 * width), jnp.float32),
+            pltpu.VMEM((lines, 2 * width), jnp.float32),
+            pltpu.VMEM((total, width), jnp.float32),
+            pltpu.VMEM(by_order.shape, jnp.float32),
+            pltpu.SemaphoreType.DMA((columns,)),
+        ]
+        + half * 4,
+        compiler_params=limit,
+        name="apply",
+    )(
+        materials,
+        jnp.full((1,), lax.axis_index("long"), jnp.int32),
+        *starts,
+        *pieces,
+        symbol_table(order),
+        np.concatenate([step, back]),
+        inverse,
+        to_orders,
+    )
+    return jnp.swapaxes(result, 1, 2)
 
 
 def solution(mesh):

time: 40 us -> 29.7 us (0.74)
  local copies, waits for them, and re-layouts: 7.52 us -> 0.07 us
  waiting for transfers between devices: 8.23 us -> 4.3 us
  other arithmetic: 0 us -> 0.67 us
  starting transfers between devices: 7.41 us -> 7.96 us
    all_to_all x1 -> x0, waiting for transfers between devices: 8.23 us -> none  [local(): lax.all_to_all(everyone, 'long', split_axis=0, concat_axis=0)]
    ppermute x0 -> x4, starting transfers between devices: none -> 7.96 us  [local(): lax.ppermute(held, 'long', [(i, i ^ distance) for i in range(devices)])]
    all_to_all x1 -> x0, starting transfers between devices: 7.41 us -> none  [local(): lax.all_to_all(everyone, 'long', split_axis=0, concat_axis=0)]
    ppermute x0 -> x4, waiting for transfers between devices: none -> 4.3 us  [local(): lax.ppermute(held, 'long', [(i, i ^ distance) for i in range(devices)])]
    unnamed x15 -> x24, local copies, waits for them, and re-layouts: 3.64 us -> 0.07 us
    pallas_call x1 -> x0, local copies, waits for them, and re-layouts: 2.44 us -> none  [local(): pl.pallas_call(panel_kernel, out_shape=jax.ShapeDtypeStruct(mode_panel.sh...]
    broadcast_in_dim x1 -> x0, local copies, waits for them, and re-layouts: 1.44 us -> none  [local(): everyone = jnp.broadcast_to(mine[None], (devices,) + mine.shape)]
    concatenate x0 -> x3, other arithmetic: none -> 0.67 us  [local(): held = jnp.concatenate(pieces, 0) if len(pieces) > 1 else mine]
  transfers between devices with their start and end apart: 1 -> 4, of which waited for: 1 -> 4; matrix products, arithmetic and copies ran while one was open for 4% -> 0% of each run, Pallas kernels for 0% -> 12%
where the time goes in v1:
time: 29.7 us; the launch traced here: 29.5 us
  Pallas kernels  16.4 us (55%)
  starting transfers between devices  7.96 us (27%)
  waiting for transfers between devices  4.3 us (14%)
  other arithmetic  0.67 us (2%)
    pallas_call x1, Pallas kernels, local(): pl.pallas_call(functools.partial(apply_kernel, groups, owners), out_shape...  10.9 us
    ppermute x4, starting transfers between devices, local(): lax.ppermute(held, 'long', [(i, i ^ distance) for i in range(devices)])  7.96 us
    ppermute x4, waiting for transfers between devices, local(): lax.ppermute(held, 'long', [(i, i ^ distance) for i in range(devices)])  4.3 us
    pallas_call x2, Pallas kernels, local(): pl.pallas_call(spread_kernel, grid=(1,), out_shape=jax.ShapeDtypeStruct((...  3.6 us
    pallas_call x1, Pallas kernels, local(): pl.pallas_call(coefficient_kernel, out_shape=jax.ShapeDtypeStruct((own, 2...  1.98 us
    concatenate x3, other arithmetic, local(): held = jnp.concatenate(pieces, 0) if len(pieces) > 1 else mine  0.67 us
  transfers between devices with their start and end apart: 4, of which 4 were waited for; matrix products, arithmetic and copies ran while one was open for 0% of the time, Pallas kernels for 12%

profile of v1, /device:TPU:0, one launch (start us, length us, event | category | flops | bytes accessed | tf_op | source)
XLA Modules:
  0.0 29.5 jit_solution(18318671163028160471)
XLA Ops:
  0.0 2.0 %coefficient.1.refs_2_ = f32[8,512]{1,0:T(8,128)} custom-call(f32[4]{0:T(128)} %mats.3, s32[8,2048]{1,0:T(8,128)} %pixels.1, bf16[2,128,512]{2,1,0:T(8,128)(2,1)} %constant.20.clone.inner, f32[16,512]{1,0:T(8,128)} %constant.21.clone.outer), custom_call_target="tpu_custom_call" | custom-call | flops 3000000000 | bytes 4194304 | tf_op jit(solution)/shard_map/coefficient/pallas_call | solution.py:320
  2.0 4.1 %collective-permute-start = (f32[8,512]{1,0:T(8,128)}, f32[8,512]{1,0:T(8,128)S(1)}, u32[]{:S(2)}, u32[]{:S(2)}) collective-permute-start(f32[8,512]{1,0:T(8,128)} %coefficient.1.refs_2_), channel_id=1, source_target_pairs={{0,8},{1,9},{2,10},{3,11},{4,12},{5,13},{6,14},{7,15},{8,0},{9,1},... | collective-permute-start | bytes 49160 | tf_op jit(solution)/shard_map/ppermute | solution.py:337
  6.1 0.0 copy-done.8
  6.1 0.0 copy-done.10
  6.1 0.0 copy-done.6
  6.1 0.0 copy-start.7
  6.1 0.0 copy-start.9
  6.1 0.0 copy-start.11
  6.1 1.8 %spread.2.refs_0_ = f32[512,256]{1,0:T(8,128)S(1)} custom-call(f32[4,201,2,201]{3,2,1,0:T(2,128)S(1)} %bitcast.3, bf16[2,256,512]{2,1,0:T(8,128)(2,1)S(1)} %copy-done.8, bf16[2,256,256]{2,1,0:T(8,128)(2,1)S(1)} %copy-done.10), custom_call_target="tpu_custom_call" | custom-call | flops 1000000000 | bytes 2097152 | tf_op jit(solution)/shard_map/spread/pallas_call | solution.py:340
  7.9 0.1 collective-permute-done.refs_3_
  8.0 0.0 copy-done.3
  8.0 0.0 copy-start.1
  8.0 0.0 copy-start.2
  8.0 0.0 copy-start.4
  8.0 0.0 copy-start.5
  8.0 2.0 %collective-permute-start.1 = (f32[16,512]{1,0:T(8,128)S(1)}, f32[16,512]{1,0:T(8,128)S(1)}, u32[]{:S(2)}, u32[]{:S(2)}) collective-permute-start(f32[16,512]{1,0:T(8,128)S(1)} %pad_maximum_fusion.2), channel_id=1, source_target_pairs={{0,4},{1,5},{2,6},{3,7},{4,0},{5,1},{6,2},{7,3},{8,12},{9,13},{10,... | collective-permute-start | bytes 98312 | tf_op jit(solution)/shard_map/ppermute | solution.py:337
  10.0 0.0 copy-done.7
  10.0 0.0 copy-done.9
  10.0 0.0 copy-done.11
  10.0 1.8 %spread.3.refs_1_ = f32[512,256]{1,0:T(8,128)S(1)} custom-call(f32[4,201,2,201]{3,2,1,0:T(2,128)S(1)} %bitcast.4, bf16[2,256,512]{2,1,0:T(8,128)(2,1)S(1)} %copy-done.9, bf16[2,256,256]{2,1,0:T(8,128)(2,1)S(1)} %copy-done.11), custom_call_target="tpu_custom_call" | custom-call | flops 1000000000 | bytes 2097152 | tf_op jit(solution)/shard_map/spread/pallas_call | solution.py:340
  11.8 0.2 collective-permute-done.1.refs_4_
  12.0 1.9 %collective-permute-start.2 = (f32[32,512]{1,0:T(8,128)S(1)}, f32[32,512]{1,0:T(8,128)S(1)}, u32[]{:S(2)}, u32[]{:S(2)}) collective-permute-start(f32[32,512]{1,0:T(8,128)S(1)} %pad_maximum_fusion.1), channel_id=1, source_target_pairs={{0,2},{1,3},{2,0},{3,1},{4,6},{5,7},{6,4},{7,5},{8,10},{9,11},{10,... | collective-permute-start | bytes 196616 | tf_op jit(solution)/shard_map/ppermute | solution.py:337
  13.9 2.4 %collective-permute-done.2.refs_5_ = f32[32,512]{1,0:T(8,128)S(1)} collective-permute-done((f32[32,512]{1,0:T(8,128)S(1)}, f32[32,512]{1,0:T(8,128)S(1)}, u32[]{:S(2)}, u32[]{:S(2)}) %collective-permute-start.2) | collective-permute-done | bytes 65568 | tf_op jit(solution)/shard_map/ppermute | solution.py:337
  16.3 0.7 %pad_maximum_fusion = f32[64,512]{1,0:T(8,128)} fusion(f32[32,512]{1,0:T(8,128)S(1)} %collective-permute-done.2.refs_5_, f32[16,512]{1,0:T(8,128)S(1)} %collective-permute-done.1.refs_4_, f32[8,512]{1,0:T(8,128)S(1)} %collective-permute-done.refs_3_, f32[8,512]{1,0:T(8,128)S(1)} %copy-done.3), kind=kLoop, calls=%fused_computation | loop fusion | flops 98304 | bytes 262144 | tf_op jit(solution)/shard_map/concatenate | solution.py:336
  17.0 0.0 collective-permute-start.3
  17.0 1.7 %collective-permute-done.3.refs_6_ = f32[64,512]{1,0:T(8,128)} collective-permute-done((f32[64,512]{1,0:T(8,128)}, f32[64,512]{1,0:T(8,128)}, u32[]{:S(2)}, u32[]{:S(2)}) %collective-permute-start.3) | collective-permute-done | bytes 131104 | tf_op jit(solution)/shard_map/ppermute | solution.py:337
  18.6 0.0 copy-done
  18.6 0.0 copy-done.1
  18.7 0.0 copy-done.2
  18.7 0.0 copy-done.4
  18.7 0.0 copy-done.5
  18.7 10.9 %apply.1 = f32[4,201,2,201]{3,2,1,0:T(2,128)} custom-call(f32[4]{0:T(128)S(1)} %copy-done.5, s32[1]{0:T(128)} %bitcast.me, f32[512,256]{1,0:T(8,128)S(1)} %spread.2.refs_0_, f32[512,256]{1,0:T(8,128)S(1)} %spread.3.refs_1_, f32[8,512]{1,0:T(8,128)S(1)} %copy-done.3, f32[8,512]{1,0:T(8,128)S(1)} %collective-permute-done.refs_3_, ...), custom_call_target="tpu_custom_call" | custom-call | tf_op jit(solution)/shard_map/apply/pallas_call | solution.py:358
  (7 shorter events, 0.0 us)
Async XLA Ops:
  0.0 6.1 %copy-start.8 = (bf16[2,256,512]{2,1,0:T(8,128)(2,1)S(1)}, bf16[2,256,512]{2,1,0:T(8,128)(2,1)}, u32[]{:S(2)}) copy-start(bf16[2,256,512]{2,1,0:T(8,128)(2,1)} %constant.22.clone.forward) | copy-start | bytes 1572868
  0.0 6.1 %copy-start.10 = (bf16[2,256,256]{2,1,0:T(8,128)(2,1)S(1)}, bf16[2,256,256]{2,1,0:T(8,128)(2,1)}, u32[]{:S(2)}) copy-start(bf16[2,256,256]{2,1,0:T(8,128)(2,1)} %constant.23.clone.to_lines) | copy-start | bytes 786436
  0.0 6.1 %copy-start.6 = (f32[4,2,201,201]{3,1,2,0:T(2,128)S(1)}, f32[4,2,201,201]{3,1,2,0:T(2,128)}, u32[]{:S(2)}) copy-start(f32[4,2,201,201]{3,1,2,0:T(2,128)} %param.13) | copy-start | bytes 3878500
  2.0 6.0 %collective-permute-start = (f32[8,512]{1,0:T(8,128)}, f32[8,512]{1,0:T(8,128)S(1)}, u32[]{:S(2)}, u32[]{:S(2)}) collective-permute-start(f32[8,512]{1,0:T(8,128)} %coefficient.1.refs_2_), channel_id=1, source_target_pairs={{0,8},{1,9},{2,10},{3,11},{4,12},{5,13},{6,14},{7,15},{8,0},{9,1},... | collective-permute-start | bytes 49160 | tf_op jit(solution)/shard_map/ppermute | solution.py:337
  6.1 1.9 %copy-start.3 = (f32[8,512]{1,0:T(8,128)S(1)}, f32[8,512]{1,0:T(8,128)}, u32[]{:S(2)}) copy-start(f32[8,512]{1,0:T(8,128)} %coefficient.1.refs_2_) | copy-start | bytes 49156
  6.1 4.0 %copy-start.7 = (f32[4,2,201,201]{3,1,2,0:T(2,128)S(1)}, f32[4,2,201,201]{3,1,2,0:T(2,128)}, u32[]{:S(2)}) copy-start(f32[4,2,201,201]{3,1,2,0:T(2,128)} %param.13) | copy-start | bytes 3878500
  6.1 3.9 %copy-start.9 = (bf16[2,256,512]{2,1,0:T(8,128)(2,1)S(1)}, bf16[2,256,512]{2,1,0:T(8,128)(2,1)}, u32[]{:S(2)}) copy-start(bf16[2,256,512]{2,1,0:T(8,128)(2,1)} %constant.22.clone.forward) | copy-start | bytes 1572868
  6.1 3.9 %copy-start.11 = (bf16[2,256,256]{2,1,0:T(8,128)(2,1)S(1)}, bf16[2,256,256]{2,1,0:T(8,128)(2,1)}, u32[]{:S(2)}) copy-start(bf16[2,256,256]{2,1,0:T(8,128)(2,1)} %constant.23.clone.to_lines) | copy-start | bytes 786436
  8.0 10.7 %copy-start = (bf16[2,512,512]{2,1,0:T(8,128)(2,1)S(1)}, bf16[2,512,512]{2,1,0:T(8,128)(2,1)}, u32[]{:S(2)}) copy-start(bf16[2,512,512]{2,1,0:T(8,128)(2,1)} %constant.24.clone.refs_7_) | copy-start | bytes 3145732
  8.0 10.7 %copy-start.1 = (bf16[2,256,512]{2,1,0:T(8,128)(2,1)S(1)}, bf16[2,256,512]{2,1,0:T(8,128)(2,1)}, u32[]{:S(2)}) copy-start(bf16[2,256,512]{2,1,0:T(8,128)(2,1)} %constant.26.clone.refs_9_) | copy-start | bytes 1572868
  8.0 10.7 %copy-start.2 = (bf16[4,256,256]{2,1,0:T(8,128)(2,1)S(1)}, bf16[4,256,256]{2,1,0:T(8,128)(2,1)}, u32[]{:S(2)}) copy-start(bf16[4,256,256]{2,1,0:T(8,128)(2,1)} %constant.25.clone.refs_8_) | copy-start | bytes 1572868
  8.0 10.6 %copy-start.4 = (bf16[2,256,256]{2,1,0:T(8,128)(2,1)S(1)}, bf16[2,256,256]{2,1,0:T(8,128)(2,1)}, u32[]{:S(2)}) copy-start(bf16[2,256,256]{2,1,0:T(8,128)(2,1)} %constant.27.clone.refs_10_) | copy-start | bytes 786436
  8.0 10.6 %copy-start.5 = (f32[4]{0:T(128)S(1)}, f32[4]{0:T(128)}, u32[]{:S(2)}) copy-start(f32[4]{0:T(128)} %mats.3) | copy-start | bytes 52
  8.0 4.0 %collective-permute-start.1 = (f32[16,512]{1,0:T(8,128)S(1)}, f32[16,512]{1,0:T(8,128)S(1)}, u32[]{:S(2)}, u32[]{:S(2)}) collective-permute-start(f32[16,512]{1,0:T(8,128)S(1)} %pad_maximum_fusion.2), channel_id=1, source_target_pairs={{0,4},{1,5},{2,6},{3,7},{4,0},{5,1},{6,2},{7,3},{8,12},{9,13},{10,... | collective-permute-start | bytes 98312 | tf_op jit(solution)/shard_map/ppermute | solution.py:337
  12.0 4.3 %collective-permute-start.2 = (f32[32,512]{1,0:T(8,128)S(1)}, f32[32,512]{1,0:T(8,128)S(1)}, u32[]{:S(2)}, u32[]{:S(2)}) collective-permute-start(f32[32,512]{1,0:T(8,128)S(1)} %pad_maximum_fusion.1), channel_id=1, source_target_pairs={{0,2},{1,3},{2,0},{3,1},{4,6},{5,7},{6,4},{7,5},{8,10},{9,11},{10,... | collective-permute-start | bytes 196616 | tf_op jit(solution)/shard_map/ppermute | solution.py:337
  17.0 1.7 %collective-permute-start.3 = (f32[64,512]{1,0:T(8,128)}, f32[64,512]{1,0:T(8,128)}, u32[]{:S(2)}, u32[]{:S(2)}) collective-permute-start(f32[64,512]{1,0:T(8,128)} %pad_maximum_fusion), channel_id=1, source_target_pairs={{0,1},{1,0},{2,3},{3,2},{4,5},{5,4},{6,7},{7,6},{8,9},{9,8},{10,11... | collective-permute-start | bytes 393224 | tf_op jit(solution)/shard_map/ppermute | solution.py:337

commit v2 on v1

--- a/solution.py
+++ b/solution.py
@@ -303,6 +303,26 @@
 VMEM = pl.BlockSpec(memory_space=pltpu.VMEM)
 
 
+def join_kernel(*refs):
+    first = 0
+    for piece in refs[:-1]:
+        refs[-1][first : first + piece.shape[0], :] = piece[...]
+        first += piece.shape[0]
+
+
+def join(pieces):
+    rows = sum(piece.shape[0] for piece in pieces)
+    return pl.pallas_call(
+        join_kernel,
+        out_shape=jax.ShapeDtypeStruct((rows, pieces[0].shape[1]), jnp.float32),
+        in_specs=[VMEM] * len(pieces),
+        out_specs=VMEM,
+        compiler_params=pltpu.CompilerParams(vmem_limit_bytes=4 * 2**20),
+        cost_estimate=pl.CostEstimate(flops=0, bytes_accessed=8 * rows * pieces[0].shape[1], transcendentals=0),
+        name="join",
+    )(*pieces)
+
+
 def local(pixel_map, materials, mode_panel):
     devices = lax.axis_size("long")
     own, npix = pixel_map.shape
@@ -314,7 +334,7 @@
     groups = 2 if columns % 2 == 0 else 1
     share = columns // groups
     total = columns * 2 * lines
-    limit = pltpu.CompilerParams(vmem_limit_bytes=24 * 2**20)
+    limit = pltpu.CompilerParams(vmem_limit_bytes=4 * 2**20)
 
     inner, outer = pixel_tables(npix, order)
     mine = pl.pallas_call(
@@ -322,6 +342,7 @@
         out_shape=jax.ShapeDtypeStruct((own, 2 * width), jnp.float32),
         in_specs=[SMEM] + [VMEM] * 3,
         out_specs=VMEM,
+        compiler_params=pltpu.CompilerParams(vmem_limit_bytes=56 * 2**20),
         cost_estimate=pl.CostEstimate(flops=3 * 10**9, bytes_accessed=2**22, transcendentals=0),
         name="coefficient",
     )(materials, pixel_map, inner, outer)
@@ -329,12 +350,16 @@
     forward, inverse, step, back = order_tables(order, 1.0 / lines)
     to_lines, to_orders = line_tables(lines, yord, rows, kept)
 
+    def exchange(block, distance):
+        return lax.ppermute(block, "long", [(i, i ^ distance) for i in range(devices)])
+
+    by_order = jnp.swapaxes(mode_panel, 1, 2)
     pieces, owners, starts = [mine], [(0,)], []
-    by_order = jnp.swapaxes(mode_panel, 1, 2)
     distance = devices // 2
-    while distance:
-        held = jnp.concatenate(pieces, 0) if len(pieces) > 1 else mine
-        other = lax.ppermute(held, "long", [(i, i ^ distance) for i in range(devices)])
+    while distance > 1:
+        held = join(pieces) if len(pieces) > 1 else mine
+        ids = tuple(d for piece in owners for d in piece)
+        other = exchange(held, distance)
         if len(starts) < groups:
             group = len(starts)
             start = pl.pallas_call(
@@ -350,8 +375,13 @@
             )(by_order, forward, to_lines)
             start, other = lax.optimization_barrier((start, other))
             starts.append(start)
-        owners.append(tuple(d ^ distance for ids in owners for d in ids))
-        pieces.append(other)
+        if distance == 2:
+            beside = exchange(held, 1)
+            pieces = [held, beside, other, exchange(other, 1)]
+            owners = [ids, tuple(d ^ 1 for d in ids), tuple(d ^ 2 for d in ids), tuple(d ^ 3 for d in ids)]
+        else:
+            pieces.append(other)
+            owners.append(tuple(d ^ distance for d in ids))
         distance //= 2
 
     half = [pltpu.VMEM((total, width), jnp.bfloat16)]
@@ -368,7 +398,8 @@
             pltpu.SemaphoreType.DMA((columns,)),
         ]
         + half * 4,
-        compiler_params=limit,
+        compiler_params=pltpu.CompilerParams(vmem_limit_bytes=10 * 2**20),
+        cost_estimate=pl.CostEstimate(flops=1000000000, bytes_accessed=4194304, transcendentals=0),
         name="apply",
     )(
         materials,

time: 29.7 us -> 28.7 us (0.966)
  other arithmetic: 0.67 us -> 0 us
    concatenate x3 -> x0, other arithmetic: 0.67 us -> none  [local(): held = jnp.concatenate(pieces, 0) if len(pieces) > 1 else mine]
    ppermute x4 -> x5, waiting for transfers between devices: 4.3 us -> 4.04 us  [exchange(): lax.ppermute(block, 'long', [(i, i ^ distance) for i in range(devices)])]
    ppermute x4 -> x5, starting transfers between devices: 7.96 us -> 7.96 us  [exchange(): lax.ppermute(block, 'long', [(i, i ^ distance) for i in range(devices)])]
  transfers between devices with their start and end apart: 4 -> 5, of which waited for: 4 -> 4; matrix products, arithmetic and copies ran while one was open for 0% -> 0% of each run, Pallas kernels for 12% -> 13%
where the time goes in v2:
time: 28.7 us; the launch traced here: 28.5 us
  Pallas kernels  16.4 us (57%)
  starting transfers between devices  7.96 us (28%)
  waiting for transfers between devices  4.04 us (14%)
    pallas_call x1, Pallas kernels, local(): pl.pallas_call(functools.partial(apply_kernel, groups, owners), out_shape...  10.8 us
    ppermute x5, starting transfers between devices, exchange(): lax.ppermute(block, 'long', [(i, i ^ distance) for i in range(devices)])  7.96 us
    ppermute x5, waiting for transfers between devices, exchange(): lax.ppermute(block, 'long', [(i, i ^ distance) for i in range(devices)])  4.04 us
    pallas_call x2, Pallas kernels, local(): pl.pallas_call(spread_kernel, grid=(1,), out_shape=jax.ShapeDtypeStruct((...  3.59 us
    pallas_call x1, Pallas kernels, local(): pl.pallas_call(coefficient_kernel, out_shape=jax.ShapeDtypeStruct((own, 2...  1.98 us
  transfers between devices with their start and end apart: 5, of which 4 were waited for; matrix products, arithmetic and copies ran while one was open for 0% of the time, Pallas kernels for 13%

profile of v2, /device:TPU:0, one launch (start us, length us, event | category | flops | bytes accessed | tf_op | source)
XLA Modules:
  0.0 28.5 jit_solution(12313828378742829530)
XLA Ops:
  0.0 0.0 copy-start.7
  0.0 0.0 copy-start.8
  0.0 0.0 copy-start.6
  0.0 2.0 %coefficient.1.refs_0_ = f32[8,512]{1,0:T(8,128)} custom-call(f32[4]{0:T(128)} %mats.3, s32[8,2048]{1,0:T(8,128)} %pixels.1, bf16[2,128,512]{2,1,0:T(8,128)(2,1)} %constant.20.clone.inner, f32[16,512]{1,0:T(8,128)} %constant.21.clone.outer), custom_call_target="tpu_custom_call" | custom-call | flops 3000000000 | bytes 4194304 | tf_op jit(solution)/shard_map/coefficient/pallas_call | solution.py:340
  2.0 4.1 %collective-permute-start = (f32[8,512]{1,0:T(8,128)}, f32[8,512]{1,0:T(8,128)S(1)}, u32[]{:S(2)}, u32[]{:S(2)}) collective-permute-start(f32[8,512]{1,0:T(8,128)} %coefficient.1.refs_0_), channel_id=1, source_target_pairs={{0,8},{1,9},{2,10},{3,11},{4,12},{5,13},{6,14},{7,15},{8,0},{9,1},... | collective-permute-start | bytes 49160 | tf_op jit(solution)/shard_map/ppermute | solution.py:354
  6.1 0.0 copy-done.7
  6.1 0.0 copy-done.8
  6.1 0.0 copy-done.6
  6.1 0.0 copy-start.4
  6.1 1.8 %spread.2.refs_0_ = f32[512,256]{1,0:T(8,128)S(1)} custom-call(f32[4,201,2,201]{3,2,1,0:T(2,128)S(1)} %bitcast.3, bf16[2,256,512]{2,1,0:T(8,128)(2,1)S(1)} %copy-done.7, bf16[2,256,256]{2,1,0:T(8,128)(2,1)S(1)} %copy-done.8), custom_call_target="tpu_custom_call" | custom-call | flops 1000000000 | bytes 2097152 | tf_op jit(solution)/shard_map/spread/pallas_call | solution.py:365
  7.9 0.1 collective-permute-done.refs_1_
  8.0 0.0 copy-done.4
  8.0 0.0 copy-start
  8.0 0.0 copy-start.1
  8.0 0.0 copy-start.2
  8.0 0.0 copy-start.3
  8.0 0.0 copy-start.5
  8.0 2.0 %collective-permute-start.1 = (f32[16,512]{1,0:T(8,128)S(1)}, f32[16,512]{1,0:T(8,128)S(1)}, u32[]{:S(2)}, u32[]{:S(2)}) collective-permute-start(f32[16,512]{1,0:T(8,128)S(1)} %join.2), channel_id=1, source_target_pairs={{0,4},{1,5},{2,6},{3,7},{4,0},{5,1},{6,2},{7,3},{8,12},{9,13},{10,... | collective-permute-start | bytes 98312 | tf_op jit(solution)/shard_map/ppermute | solution.py:354
  10.0 1.8 %spread.3.refs_1_ = f32[512,256]{1,0:T(8,128)S(1)} custom-call(f32[4,201,2,201]{3,2,1,0:T(2,128)S(1)} %bitcast.4, bf16[2,256,512]{2,1,0:T(8,128)(2,1)S(1)} %copy-done.7, bf16[2,256,256]{2,1,0:T(8,128)(2,1)S(1)} %copy-done.8), custom_call_target="tpu_custom_call" | custom-call | flops 1000000000 | bytes 2097152 | tf_op jit(solution)/shard_map/spread/pallas_call | solution.py:365
  11.8 0.2 collective-permute-done.1.refs_2_
  12.0 1.9 %collective-permute-start.3 = (f32[32,512]{1,0:T(8,128)S(1)}, f32[32,512]{1,0:T(8,128)S(1)}, u32[]{:S(2)}, u32[]{:S(2)}) collective-permute-start(f32[32,512]{1,0:T(8,128)S(1)} %join.3.refs_2_), channel_id=1, source_target_pairs={{0,2},{1,3},{2,0},{3,1},{4,6},{5,7},{6,4},{7,5},{8,10},{9,11},{10,... | collective-permute-start | bytes 196616 | tf_op jit(solution)/shard_map/ppermute | solution.py:354
  13.9 0.0 collective-permute-start.2
  13.9 2.4 %collective-permute-done.3.refs_4_ = f32[32,512]{1,0:T(8,128)S(1)} collective-permute-done((f32[32,512]{1,0:T(8,128)S(1)}, f32[32,512]{1,0:T(8,128)S(1)}, u32[]{:S(2)}, u32[]{:S(2)}) %collective-permute-start.3) | collective-permute-done | bytes 65568 | tf_op jit(solution)/shard_map/ppermute | solution.py:354
  16.3 0.0 collective-permute-start.4
  16.3 0.0 collective-permute-done.2.refs_3_
  16.3 1.4 %collective-permute-done.4.refs_5_ = f32[32,512]{1,0:T(8,128)} collective-permute-done((f32[32,512]{1,0:T(8,128)S(1)}, f32[32,512]{1,0:T(8,128)}, u32[]{:S(2)}, u32[]{:S(2)}) %collective-permute-start.4) | collective-permute-done | bytes 65568 | tf_op jit(solution)/shard_map/ppermute | solution.py:354
  17.7 0.0 copy-done
  17.7 0.0 copy-done.1
  17.7 0.0 copy-done.2
  17.7 0.0 copy-done.3
  17.7 0.0 copy-done.5
  17.7 10.8 %apply.1 = f32[4,201,2,201]{3,2,1,0:T(2,128)} custom-call(f32[4]{0:T(128)S(1)} %copy-done.5, s32[1]{0:T(128)} %bitcast.me, f32[512,256]{1,0:T(8,128)S(1)} %spread.2.refs_0_, f32[512,256]{1,0:T(8,128)S(1)} %spread.3.refs_1_, f32[32,512]{1,0:T(8,128)S(1)} %join.3.refs_2_, f32[32,512]{1,0:T(8,128)} %collective-permute-done.2.refs_3_, ...), custom_call_target="tpu_custom_call" | custom-call | flops 1000000000 | bytes 4194304 | tf_op jit(solution)/shard_map/apply/pallas_call | solution.py:388
  (2 shorter events, 0.0 us)
Async XLA Ops:
  0.0 6.1 %copy-start.7 = (bf16[2,256,512]{2,1,0:T(8,128)(2,1)S(1)}, bf16[2,256,512]{2,1,0:T(8,128)(2,1)}, u32[]{:S(2)}) copy-start(bf16[2,256,512]{2,1,0:T(8,128)(2,1)} %constant.22.clone.forward) | copy-start | bytes 1572868
  0.0 6.1 %copy-start.8 = (bf16[2,256,256]{2,1,0:T(8,128)(2,1)S(1)}, bf16[2,256,256]{2,1,0:T(8,128)(2,1)}, u32[]{:S(2)}) copy-start(bf16[2,256,256]{2,1,0:T(8,128)(2,1)} %constant.23.clone.to_lines) | copy-start | bytes 786436
  0.0 6.1 %copy-start.6 = (f32[4,2,201,201]{3,1,2,0:T(2,128)S(1)}, f32[4,2,201,201]{3,1,2,0:T(2,128)}, u32[]{:S(2)}) copy-start(f32[4,2,201,201]{3,1,2,0:T(2,128)} %param.13) | copy-start | bytes 3878500
  2.0 6.0 %collective-permute-start = (f32[8,512]{1,0:T(8,128)}, f32[8,512]{1,0:T(8,128)S(1)}, u32[]{:S(2)}, u32[]{:S(2)}) collective-permute-start(f32[8,512]{1,0:T(8,128)} %coefficient.1.refs_0_), channel_id=1, source_target_pairs={{0,8},{1,9},{2,10},{3,11},{4,12},{5,13},{6,14},{7,15},{8,0},{9,1},... | collective-permute-start | bytes 49160 | tf_op jit(solution)/shard_map/ppermute | solution.py:354
  6.1 1.9 %copy-start.4 = (f32[8,512]{1,0:T(8,128)S(1)}, f32[8,512]{1,0:T(8,128)}, u32[]{:S(2)}) copy-start(f32[8,512]{1,0:T(8,128)} %coefficient.1.refs_0_) | copy-start | bytes 49156
  8.0 9.7 %copy-start = (bf16[2,512,512]{2,1,0:T(8,128)(2,1)S(1)}, bf16[2,512,512]{2,1,0:T(8,128)(2,1)}, u32[]{:S(2)}) copy-start(bf16[2,512,512]{2,1,0:T(8,128)(2,1)} %constant.24.clone.refs_6_) | copy-start | bytes 3145732
  8.0 9.7 %copy-start.1 = (bf16[2,256,512]{2,1,0:T(8,128)(2,1)S(1)}, bf16[2,256,512]{2,1,0:T(8,128)(2,1)}, u32[]{:S(2)}) copy-start(bf16[2,256,512]{2,1,0:T(8,128)(2,1)} %constant.26.clone.refs_8_) | copy-start | bytes 1572868
  8.0 9.7 %copy-start.2 = (bf16[4,256,256]{2,1,0:T(8,128)(2,1)S(1)}, bf16[4,256,256]{2,1,0:T(8,128)(2,1)}, u32[]{:S(2)}) copy-start(bf16[4,256,256]{2,1,0:T(8,128)(2,1)} %constant.25.clone.refs_7_) | copy-start | bytes 1572868
  8.0 9.7 %copy-start.3 = (bf16[2,256,256]{2,1,0:T(8,128)(2,1)S(1)}, bf16[2,256,256]{2,1,0:T(8,128)(2,1)}, u32[]{:S(2)}) copy-start(bf16[2,256,256]{2,1,0:T(8,128)(2,1)} %constant.27.clone.refs_9_) | copy-start | bytes 786436
  8.0 9.7 %copy-start.5 = (f32[4]{0:T(128)S(1)}, f32[4]{0:T(128)}, u32[]{:S(2)}) copy-start(f32[4]{0:T(128)} %mats.3) | copy-start | bytes 52
  8.0 4.0 %collective-permute-start.1 = (f32[16,512]{1,0:T(8,128)S(1)}, f32[16,512]{1,0:T(8,128)S(1)}, u32[]{:S(2)}, u32[]{:S(2)}) collective-permute-start(f32[16,512]{1,0:T(8,128)S(1)} %join.2), channel_id=1, source_target_pairs={{0,4},{1,5},{2,6},{3,7},{4,0},{5,1},{6,2},{7,3},{8,12},{9,13},{10,... | collective-permute-start | bytes 98312 | tf_op jit(solution)/shard_map/ppermute | solution.py:354
  12.0 4.3 %collective-permute-start.3 = (f32[32,512]{1,0:T(8,128)S(1)}, f32[32,512]{1,0:T(8,128)S(1)}, u32[]{:S(2)}, u32[]{:S(2)}) collective-permute-start(f32[32,512]{1,0:T(8,128)S(1)} %join.3.refs_2_), channel_id=1, source_target_pairs={{0,2},{1,3},{2,0},{3,1},{4,6},{5,7},{6,4},{7,5},{8,10},{9,11},{10,... | collective-permute-start | bytes 196616 | tf_op jit(solution)/shard_map/ppermute | solution.py:354
  13.9 2.4 %collective-permute-start.2 = (f32[32,512]{1,0:T(8,128)S(1)}, f32[32,512]{1,0:T(8,128)}, u32[]{:S(2)}, u32[]{:S(2)}) collective-permute-start(f32[32,512]{1,0:T(8,128)S(1)} %join.3.refs_2_), channel_id=1, source_target_pairs={{0,1},{1,0},{2,3},{3,2},{4,5},{5,4},{6,7},{7,6},{8,9},{9,8},{10,11... | collective-permute-start | bytes 196616 | tf_op jit(solution)/shard_map/ppermute | solution.py:354
  16.3 1.4 %collective-permute-start.4 = (f32[32,512]{1,0:T(8,128)S(1)}, f32[32,512]{1,0:T(8,128)}, u32[]{:S(2)}, u32[]{:S(2)}) collective-permute-start(f32[32,512]{1,0:T(8,128)S(1)} %collective-permute-done.3.refs_4_), channel_id=1, source_target_pairs={{0,1},{1,0},{2,3},{3,2},{4,5},{5,4},{6,7},{7,6},{8,9},{9,8},{10,11... | collective-permute-start | bytes 196616 | tf_op jit(solution)/shard_map/ppermute | solution.py:354

commit v3 on v2

--- a/solution.py
+++ b/solution.py
@@ -13,6 +13,7 @@
 NS_ITERS = 3
 LANES = 128
 BLOCK = 128
+SUM_ROWS = 1024
 
 
 def up(value, step):
@@ -159,7 +160,7 @@
         out[c * double_lines : (c + 1) * double_lines, :] = value
 
 
-def sweeps(count, half, start_of, symbol, steps, state, now, other, sums):
+def sweeps(count, half, start_of, first_of, symbol, steps, state, now, other, sums, done):
     lines, width = symbol.shape[0], state.shape[1]
     blocks = half // BLOCK
     per_section = blocks // 2
@@ -187,7 +188,13 @@
                 load = 1 if block == own[0] else None
                 pltpu.matmul_acc_lhs(sums[unit * blocks + block], high[rows(unit, block)], load_staged_rhs=load)
 
-    def finish(stage, section):
+    def first_product(section):
+        for block in range(section * per_section, (section + 1) * per_section):
+            for unit in range(2):
+                place = rows(unit, block)
+                other[0][place], other[1][place] = split(first_of(unit, block) * symbol_rows(unit, block, 1))
+
+    def finish(stage, section, first=False):
         for block in range(section * per_section, (section + 1) * per_section):
             for unit in range(2):
                 place = rows(unit, block)
@@ -196,7 +203,9 @@
                     high, low = split(value * symbol_rows(unit, block, 1))
                     other[0][place], other[1][place] = high, low
                 else:
-                    value = start_of(unit, block) + state[place] * symbol_rows(unit, block, 0) + value
+                    start = start_of(unit, block)
+                    held = start if first else state[place]
+                    value = start + held * symbol_rows(unit, block, 0) + value
                     state[place] = value
                     now[0][place], now[1][place] = split(value)
 
@@ -208,10 +217,29 @@
             elif not last:
                 issue(*order[0])
             finish(*unit)
-
+            if last and unit[0] == 1:
+                done(unit[1])
+
+    for section in range(2):
+        first_product(section)
+        issue(1, section)
+    finish(1, 0, first=True)
     issue(0, 0)
-    lax.fori_loop(0, count - 1, lambda _, carry: (sweep(False), carry)[1], 0)
+    finish(1, 1, first=True)
+    lax.fori_loop(0, count - 2, lambda _, carry: (sweep(False), carry)[1], 0)
     sweep(True)
+
+
+def product_kernel(*refs):
+    sources, step, both, out = refs[:-3], refs[-3], refs[-2], refs[-1]
+    rows = sources[0].shape[0]
+    for i, source in enumerate(sources):
+        for first in range(0, rows, 2 * BLOCK):
+            place = slice(first, first + 2 * BLOCK)
+            value = source[place, :]
+            target = slice(i * rows + first, i * rows + first + 2 * BLOCK)
+            both[target, :] = value
+            out[target, :] = dot_split(split(value), pair(step))
 
 
 def unit_product(lhs, rhs, unit, sums):
@@ -227,8 +255,8 @@
     return pltpu.matmul_pop(sums)
 
 
-def apply_kernel(groups, owners, mats, me, *refs):
-    starts, refs = refs[:groups], refs[groups:]
+def apply_kernel(owners, mats, start, product, *refs):
+    me = lax.axis_index("long")
     pieces, refs = refs[: len(owners)], refs[len(owners) :]
     table, steps, inverse, to_orders, out, coefficients, symbol, state, result, ready, *splits = refs
     now, other = splits[:2], splits[2:]
@@ -242,7 +270,7 @@
     for piece, ids in zip(pieces, owners):
         own = piece.shape[0] // len(ids)
         for index, distance in enumerate(ids):
-            place = pl.multiple_of((me[0] ^ distance) * own, own)
+            place = pl.multiple_of((me ^ distance) * own, own)
             coefficients[pl.ds(place, own), :] = piece[index * own : (index + 1) * own]
     values = split(coefficients[...])
 
@@ -254,49 +282,57 @@
 
     pl.run_scoped(all_symbols, *[pltpu.ACC(unit)((lines, width), jnp.float32) for unit in range(2)])
 
-    share = state.shape[0] // groups
-    for group in range(groups):
-        place = slice(group * share, (group + 1) * share)
-        value = starts[group][...]
-        state[place] = value
-        now[0][place], now[1][place] = split(value)
-
     def start_of(unit, block):
         first = unit * half + block * BLOCK
-        return starts[first // share][first % share : first % share + BLOCK]
+        return start[first : first + BLOCK]
+
+    def first_of(unit, block):
+        first = unit * half + block * BLOCK
+        return product[first : first + BLOCK]
+
+    def to_panel(c, sums):
+        place = slice(c * 2 * lines, (c + 1) * 2 * lines)
+        unit = c * 2 * lines // half
+        value = unit_product((to_orders[0], to_orders[1]), (now[0].at[place], now[1].at[place]), unit, sums[unit])
+        value = split(value * factor)
+        cosine, sine = (
+            unit_product(
+                value,
+                tuple(inverse.at[part, :, unit * width : (unit + 1) * width] for part in range(2)),
+                unit,
+                sums[2 + unit],
+            )
+            for unit in range(2)
+        )
+        real = cosine[:rows] - sine[rows:]
+        imag = cosine[rows:] + sine[:rows]
+        for part, value in enumerate((real, imag)):
+            for first in range(0, yord, lines):
+                count = min(lines, yord - first)
+                result[c, first : first + count, part, :] = value[:count, :order]
+        pltpu.make_async_copy(result.at[c], out.at[c], ready.at[c]).start()
+
+    early = columns % 4 == 0 and half + 4 * rows <= SUM_ROWS
 
     def run(*sums):
-        sweeps(2**NS_ITERS - 1, half, start_of, symbol, steps, state, now, other, sums)
-
-    pl.run_scoped(run, *[pltpu.ACC(unit)((BLOCK, width), jnp.float32) for unit in range(2) for _ in range(half // BLOCK)])
-
-    def finish(*sums):
-        for c in range(columns):
-            place = slice(c * 2 * lines, (c + 1) * 2 * lines)
-            data = now[0].at[place], now[1].at[place]
-            value = unit_product((to_orders[0], to_orders[1]), data, c % 2, sums[c % 2])
-            value = split(value * factor)
-            cosine, sine = (
-                unit_product(
-                    value,
-                    tuple(inverse.at[part, :, unit * width : (unit + 1) * width] for part in range(2)),
-                    unit,
-                    sums[2 + 2 * (c % buffers) + unit],
-                )
-                for unit in range(2)
-            )
-            real = cosine[:rows] - sine[rows:]
-            imag = cosine[rows:] + sine[:rows]
-            for part, value in enumerate((real, imag)):
-                for first in range(0, yord, lines):
-                    count = min(lines, yord - first)
-                    result[c, first : first + count, part, :] = value[:count, :order]
-            pltpu.make_async_copy(result.at[c], out.at[c], ready.at[c]).start()
-        for c in range(columns):
-            pltpu.make_async_copy(result.at[c], out.at[c], ready.at[c]).wait()
-
-    buffers = min(2, columns)
-    pl.run_scoped(finish, *[pltpu.ACC(i % 2)((2 * rows, width), jnp.float32) for i in range(2 + 2 * buffers)])
+        blocks = 2 * (half // BLOCK)
+
+        def done(section):
+            if early:
+                quarter = columns // 4
+                for c in range(quarter):
+                    for unit in range(2):
+                        to_panel((2 * unit + section) * quarter + c, sums[blocks:])
+
+        sweeps(2**NS_ITERS - 1, half, start_of, first_of, symbol, steps, state, now, other, sums[:blocks], done)
+
+    sum_types = [pltpu.ACC(i % 2)((2 * rows, width), jnp.float32) for i in range(4)]
+    block_types = [pltpu.ACC(unit)((BLOCK, width), jnp.float32) for unit in range(2) for _ in range(half // BLOCK)]
+    pl.run_scoped(run, *block_types, *(sum_types if early else []))
+    if not early:
+        pl.run_scoped(lambda *sums: [to_panel(c, sums) for c in range(columns)] and None, *sum_types)
+    for c in range(columns):
+        pltpu.make_async_copy(result.at[c], out.at[c], ready.at[c]).wait()
 
 
 SMEM = pl.BlockSpec(memory_space=pltpu.SMEM)
@@ -376,6 +412,16 @@
             start, other = lax.optimization_barrier((start, other))
             starts.append(start)
         if distance == 2:
+            start, product = pl.pallas_call(
+                product_kernel,
+                out_shape=[jax.ShapeDtypeStruct((total, width), jnp.float32)] * 2,
+                in_specs=[VMEM] * (groups + 1),
+                out_specs=[VMEM] * 2,
+                compiler_params=limit,
+                cost_estimate=pl.CostEstimate(flops=10**9, bytes_accessed=2**21, transcendentals=0),
+                name="product",
+            )(*starts, step)
+            start, product, other = lax.optimization_barrier((start, product, other))
             beside = exchange(held, 1)
             pieces = [held, beside, other, exchange(other, 1)]
             owners = [ids, tuple(d ^ 1 for d in ids), tuple(d ^ 2 for d in ids), tuple(d ^ 3 for d in ids)]
@@ -386,9 +432,9 @@
 
     half = [pltpu.VMEM((total, width), jnp.bfloat16)]
     result = pl.pallas_call(
-        functools.partial(apply_kernel, groups, owners),
+        functools.partial(apply_kernel, owners),
         out_shape=jax.ShapeDtypeStruct(by_order.shape, jnp.float32),
-        in_specs=[SMEM, SMEM] + [VMEM] * (4 + groups + len(pieces)),
+        in_specs=[SMEM] + [VMEM] * (6 + len(pieces)),
         out_specs=pl.BlockSpec(memory_space=pl.ANY),
         scratch_shapes=[
             pltpu.VMEM((lines, 2 * width), jnp.float32),
@@ -403,8 +449,8 @@
         name="apply",
     )(
         materials,
-        jnp.full((1,), lax.axis_index("long"), jnp.int32),
-        *starts,
+        start,
+        product,
         *pieces,
         symbol_table(order),
         np.concatenate([step, back]),

time: 28.7 us -> 28.4 us (0.990)
  waiting for transfers between devices: 4.04 us -> 3.62 us
    ppermute x5, waiting for transfers between devices: 4.04 us -> 3.62 us  [exchange(): lax.ppermute(block, 'long', [(i, i ^ distance) for i in range(devices)])]
    pallas_call x1 -> x2, Pallas kernels: 10.8 us -> 10.8 us  [the longest x1 10.2 us: local(): pl.pallas_call(functools.partial(apply_kernel, owners), out_shape=jax.Sha...]
  transfers between devices with their start and end apart: 5 -> 5, of which waited for: 4 -> 4; matrix products, arithmetic and copies ran while one was open for 0% -> 0% of each run, Pallas kernels for 13% -> 15%
where the time goes in v3:
time: 28.4 us; the launch traced here: 28.2 us
  Pallas kernels  16.4 us (58%)
  starting transfers between devices  8.09 us (28%)
  waiting for transfers between devices  3.62 us (13%)
    pallas_call x1, Pallas kernels, local(): pl.pallas_call(functools.partial(apply_kernel, owners), out_shape=jax.Sha...  10.2 us
    ppermute x5, starting transfers between devices, exchange(): lax.ppermute(block, 'long', [(i, i ^ distance) for i in range(devices)])  8.09 us
    ppermute x5, waiting for transfers between devices, exchange(): lax.ppermute(block, 'long', [(i, i ^ distance) for i in range(devices)])  3.62 us
    pallas_call x2, Pallas kernels, local(): pl.pallas_call(spread_kernel, grid=(1,), out_shape=jax.ShapeDtypeStruct((...  3.59 us
    pallas_call x1, Pallas kernels, local(): pl.pallas_call(coefficient_kernel, out_shape=jax.ShapeDtypeStruct((own, 2...  1.98 us
    pallas_call x1, Pallas kernels, local(): pl.pallas_call(product_kernel, out_shape=[jax.ShapeDtypeStruct((total, wi...  0.6 us
  transfers between devices with their start and end apart: 5, of which 4 were waited for; matrix products, arithmetic and copies ran while one was open for 0% of the time, Pallas kernels for 15%

profile of v3, /device:TPU:0, one launch (start us, length us, event | category | flops | bytes accessed | tf_op | source)
XLA Modules:
  0.0 28.2 jit_solution(6158390359667957440)
XLA Ops:
  0.0 0.0 copy-start.7
  0.0 0.0 copy-start.9
  0.0 0.0 copy-start.6
  0.0 2.0 %coefficient.1.refs_0_ = f32[8,512]{1,0:T(8,128)} custom-call(f32[4]{0:T(128)} %mats.3, s32[8,2048]{1,0:T(8,128)} %pixels.1, bf16[2,128,512]{2,1,0:T(8,128)(2,1)} %constant.18.clone.inner, f32[16,512]{1,0:T(8,128)} %constant.19.clone.outer), custom_call_target="tpu_custom_call" | custom-call | flops 3000000000 | bytes 4194304 | tf_op jit(solution)/shard_map/coefficient/pallas_call | solution.py:376
  2.0 4.1 %collective-permute-start = (f32[8,512]{1,0:T(8,128)}, f32[8,512]{1,0:T(8,128)S(1)}, u32[]{:S(2)}, u32[]{:S(2)}) collective-permute-start(f32[8,512]{1,0:T(8,128)} %coefficient.1.refs_0_), channel_id=1, source_target_pairs={{0,8},{1,9},{2,10},{3,11},{4,12},{5,13},{6,14},{7,15},{8,0},{9,1},... | collective-permute-start | bytes 49160 | tf_op jit(solution)/shard_map/ppermute | solution.py:390
  6.1 0.0 copy-done.7
  6.1 0.0 copy-done.9
  6.1 0.0 copy-done.6
  6.1 1.8 %spread.2.refs_0_ = f32[512,256]{1,0:T(8,128)S(1)} custom-call(f32[4,201,2,201]{3,2,1,0:T(2,128)S(1)} %bitcast.2, bf16[2,256,512]{2,1,0:T(8,128)(2,1)S(1)} %copy-done.7, bf16[2,256,256]{2,1,0:T(8,128)(2,1)S(1)} %copy-done.9), custom_call_target="tpu_custom_call" | custom-call | flops 1000000000 | bytes 2097152 | tf_op jit(solution)/shard_map/spread/pallas_call | solution.py:401
  7.9 0.1 collective-permute-done.refs_1_
  8.0 0.0 copy-done.4
  8.0 2.0 %collective-permute-start.1 = (f32[16,512]{1,0:T(8,128)S(1)}, f32[16,512]{1,0:T(8,128)S(1)}, u32[]{:S(2)}, u32[]{:S(2)}) collective-permute-start(f32[16,512]{1,0:T(8,128)S(1)} %join.2), channel_id=1, source_target_pairs={{0,4},{1,5},{2,6},{3,7},{4,0},{5,1},{6,2},{7,3},{8,12},{9,13},{10,... | collective-permute-start | bytes 98312 | tf_op jit(solution)/shard_map/ppermute | solution.py:390
  10.0 1.8 %spread.3.refs_1_ = f32[512,256]{1,0:T(8,128)S(1)} custom-call(f32[4,201,2,201]{3,2,1,0:T(2,128)S(1)} %bitcast.3, bf16[2,256,512]{2,1,0:T(8,128)(2,1)S(1)} %copy-done.7, bf16[2,256,256]{2,1,0:T(8,128)(2,1)S(1)} %copy-done.9), custom_call_target="tpu_custom_call" | custom-call | flops 1000000000 | bytes 2097152 | tf_op jit(solution)/shard_map/spread/pallas_call | solution.py:401
  11.8 0.2 collective-permute-done.1.refs_2_
  12.0 0.0 copy-start.1
  12.0 0.0 copy-start.2
  12.0 0.0 copy-start.3
  12.0 0.0 copy-start.5
  12.0 0.1 collective-permute-start.3
  12.1 2.0 %collective-permute-start.2 = (f32[32,512]{1,0:T(8,128)S(1)}, f32[32,512]{1,0:T(8,128)S(1)}, u32[]{:S(2)}, u32[]{:S(2)}) collective-permute-start(f32[32,512]{1,0:T(8,128)S(1)} %join.3.refs_0_), channel_id=1, source_target_pairs={{0,2},{1,3},{2,0},{3,1},{4,6},{5,7},{6,4},{7,5},{8,10},{9,11},{10,... | collective-permute-start | bytes 196616 | tf_op jit(solution)/shard_map/ppermute | solution.py:390
  14.1 0.0 copy-done.8
  14.1 0.6 %product.1 = (f32[1024,256]{1,0:T(8,128)S(1)}, f32[1024,256]{1,0:T(8,128)S(1)}) custom-call(f32[512,256]{1,0:T(8,128)S(1)} %spread.2.refs_0_, f32[512,256]{1,0:T(8,128)S(1)} %spread.3.refs_1_, bf16[2,256,256]{2,1,0:T(8,128)(2,1)S(1)} %copy-done.8), custom_call_target="tpu_custom_call" | custom-call | flops 1000000000 | bytes 2097152 | tf_op jit(solution)/shard_map/product/pallas_call | solution.py:415
  14.7 2.1 %collective-permute-done.2.refs_2_ = f32[32,512]{1,0:T(8,128)S(1)} collective-permute-done((f32[32,512]{1,0:T(8,128)S(1)}, f32[32,512]{1,0:T(8,128)S(1)}, u32[]{:S(2)}, u32[]{:S(2)}) %collective-permute-start.2) | collective-permute-done | bytes 65568 | tf_op jit(solution)/shard_map/ppermute | solution.py:390
  16.8 0.0 collective-permute-start.4
  16.8 0.0 collective-permute-done.3.refs_1_
  16.8 1.2 %collective-permute-done.4.refs_3_ = f32[32,512]{1,0:T(8,128)S(1)} collective-permute-done((f32[32,512]{1,0:T(8,128)S(1)}, f32[32,512]{1,0:T(8,128)S(1)}, u32[]{:S(2)}, u32[]{:S(2)}) %collective-permute-start.4) | collective-permute-done | bytes 65568 | tf_op jit(solution)/shard_map/ppermute | solution.py:390
  18.0 0.0 copy-done
  18.0 0.0 copy-done.1
  18.0 0.0 copy-done.2
  18.0 0.0 copy-done.3
  18.0 0.0 copy-done.5
  18.1 10.2 %apply.1 = f32[4,201,2,201]{3,2,1,0:T(2,128)} custom-call(f32[4]{0:T(128)S(1)} %copy-done.5, f32[1024,256]{1,0:T(8,128)S(1)} %get-tuple-element.20.start, f32[1024,256]{1,0:T(8,128)S(1)} %get-tuple-element.21.product, f32[32,512]{1,0:T(8,128)S(1)} %join.3.refs_0_, f32[32,512]{1,0:T(8,128)S(1)} %collective-permute-done.3.refs_1_, ...), custom_call_target="tpu_custom_call" | custom-call | flops 1000000000 | bytes 4194304 | tf_op jit(solution)/shard_map/apply/pallas_call | solution.py:434
  (5 shorter events, 0.0 us)
Async XLA Ops:
  0.0 6.1 %copy-start.7 = (bf16[2,256,512]{2,1,0:T(8,128)(2,1)S(1)}, bf16[2,256,512]{2,1,0:T(8,128)(2,1)}, u32[]{:S(2)}) copy-start(bf16[2,256,512]{2,1,0:T(8,128)(2,1)} %constant.20.clone.forward) | copy-start | bytes 1572868
  0.0 6.1 %copy-start.9 = (bf16[2,256,256]{2,1,0:T(8,128)(2,1)S(1)}, bf16[2,256,256]{2,1,0:T(8,128)(2,1)}, u32[]{:S(2)}) copy-start(bf16[2,256,256]{2,1,0:T(8,128)(2,1)} %constant.21.clone.to_lines) | copy-start | bytes 786436
  0.0 6.1 %copy-start.6 = (f32[4,2,201,201]{3,1,2,0:T(2,128)S(1)}, f32[4,2,201,201]{3,1,2,0:T(2,128)}, u32[]{:S(2)}) copy-start(f32[4,2,201,201]{3,1,2,0:T(2,128)} %param.14) | copy-start | bytes 3878500
  2.0 6.0 %collective-permute-start = (f32[8,512]{1,0:T(8,128)}, f32[8,512]{1,0:T(8,128)S(1)}, u32[]{:S(2)}, u32[]{:S(2)}) collective-permute-start(f32[8,512]{1,0:T(8,128)} %coefficient.1.refs_0_), channel_id=1, source_target_pairs={{0,8},{1,9},{2,10},{3,11},{4,12},{5,13},{6,14},{7,15},{8,0},{9,1},... | collective-permute-start | bytes 49160 | tf_op jit(solution)/shard_map/ppermute | solution.py:390
  6.1 1.9 %copy-start.4 = (f32[8,512]{1,0:T(8,128)S(1)}, f32[8,512]{1,0:T(8,128)}, u32[]{:S(2)}) copy-start(f32[8,512]{1,0:T(8,128)} %coefficient.1.refs_0_) | copy-start | bytes 49156
  8.0 6.1 %copy-start.8 = (bf16[2,256,256]{2,1,0:T(8,128)(2,1)S(1)}, bf16[2,256,256]{2,1,0:T(8,128)(2,1)}, u32[]{:S(2)}) copy-start(bf16[2,256,256]{2,1,0:T(8,128)(2,1)} %constant.22.clone.refs_2_) | copy-start | bytes 786436
  8.0 4.0 %collective-permute-start.1 = (f32[16,512]{1,0:T(8,128)S(1)}, f32[16,512]{1,0:T(8,128)S(1)}, u32[]{:S(2)}, u32[]{:S(2)}) collective-permute-start(f32[16,512]{1,0:T(8,128)S(1)} %join.2), channel_id=1, source_target_pairs={{0,4},{1,5},{2,6},{3,7},{4,0},{5,1},{6,2},{7,3},{8,12},{9,13},{10,... | collective-permute-start | bytes 98312 | tf_op jit(solution)/shard_map/ppermute | solution.py:390
  12.0 6.1 %copy-start = (bf16[2,512,512]{2,1,0:T(8,128)(2,1)S(1)}, bf16[2,512,512]{2,1,0:T(8,128)(2,1)}, u32[]{:S(2)}) copy-start(bf16[2,512,512]{2,1,0:T(8,128)(2,1)} %constant.23.clone.refs_4_) | copy-start | bytes 3145732
  12.0 6.0 %copy-start.1 = (bf16[2,256,512]{2,1,0:T(8,128)(2,1)S(1)}, bf16[2,256,512]{2,1,0:T(8,128)(2,1)}, u32[]{:S(2)}) copy-start(bf16[2,256,512]{2,1,0:T(8,128)(2,1)} %constant.25.clone.refs_6_) | copy-start | bytes 1572868
  12.0 6.0 %copy-start.2 = (bf16[4,256,256]{2,1,0:T(8,128)(2,1)S(1)}, bf16[4,256,256]{2,1,0:T(8,128)(2,1)}, u32[]{:S(2)}) copy-start(bf16[4,256,256]{2,1,0:T(8,128)(2,1)} %constant.24.clone.refs_5_) | copy-start | bytes 1572868
  12.0 6.0 %copy-start.3 = (bf16[2,256,256]{2,1,0:T(8,128)(2,1)S(1)}, bf16[2,256,256]{2,1,0:T(8,128)(2,1)}, u32[]{:S(2)}) copy-start(bf16[2,256,256]{2,1,0:T(8,128)(2,1)} %constant.26.clone.refs_7_) | copy-start | bytes 786436
  12.0 6.0 %copy-start.5 = (f32[4]{0:T(128)S(1)}, f32[4]{0:T(128)}, u32[]{:S(2)}) copy-start(f32[4]{0:T(128)} %mats.3) | copy-start | bytes 52
  12.0 4.7 %collective-permute-start.3 = (f32[32,512]{1,0:T(8,128)S(1)}, f32[32,512]{1,0:T(8,128)S(1)}, u32[]{:S(2)}, u32[]{:S(2)}) collective-permute-start(f32[32,512]{1,0:T(8,128)S(1)} %join.3.refs_0_), channel_id=1, source_target_pairs={{0,1},{1,0},{2,3},{3,2},{4,5},{5,4},{6,7},{7,6},{8,9},{9,8},{10,11... | collective-permute-start | bytes 196616 | tf_op jit(solution)/shard_map/ppermute | solution.py:390
  12.1 4.7 %collective-permute-start.2 = (f32[32,512]{1,0:T(8,128)S(1)}, f32[32,512]{1,0:T(8,128)S(1)}, u32[]{:S(2)}, u32[]{:S(2)}) collective-permute-start(f32[32,512]{1,0:T(8,128)S(1)} %join.3.refs_0_), channel_id=1, source_target_pairs={{0,2},{1,3},{2,0},{3,1},{4,6},{5,7},{6,4},{7,5},{8,10},{9,11},{10,... | collective-permute-start | bytes 196616 | tf_op jit(solution)/shard_map/ppermute | solution.py:390
  16.8 1.3 %collective-permute-start.4 = (f32[32,512]{1,0:T(8,128)S(1)}, f32[32,512]{1,0:T(8,128)S(1)}, u32[]{:S(2)}, u32[]{:S(2)}) collective-permute-start(f32[32,512]{1,0:T(8,128)S(1)} %collective-permute-done.2.refs_2_), channel_id=1, source_target_pairs={{0,1},{1,0},{2,3},{3,2},{4,5},{5,4},{6,7},{7,6},{8,9},{9,8},{10,11... | collective-permute-start | bytes 196616 | tf_op jit(solution)/shard_map/ppermute | solution.py:390

commit v4 on v3

--- a/solution.py
+++ b/solution.py
@@ -13,7 +13,6 @@
 NS_ITERS = 3
 LANES = 128
 BLOCK = 128
-SUM_ROWS = 1024
 
 
 def up(value, step):
@@ -160,7 +159,7 @@
         out[c * double_lines : (c + 1) * double_lines, :] = value
 
 
-def sweeps(count, half, start_of, first_of, symbol, steps, state, now, other, sums, done):
+def sweeps(count, half, start_of, first_of, symbol, steps, state, now, other, sums):
     lines, width = symbol.shape[0], state.shape[1]
     blocks = half // BLOCK
     per_section = blocks // 2
@@ -193,8 +192,9 @@
             for unit in range(2):
                 place = rows(unit, block)
                 other[0][place], other[1][place] = split(first_of(unit, block) * symbol_rows(unit, block, 1))
-
-    def finish(stage, section, first=False):
+                state[place] = start_of(unit, block)
+
+    def finish(stage, section):
         for block in range(section * per_section, (section + 1) * per_section):
             for unit in range(2):
                 place = rows(unit, block)
@@ -203,31 +203,27 @@
                     high, low = split(value * symbol_rows(unit, block, 1))
                     other[0][place], other[1][place] = high, low
                 else:
-                    start = start_of(unit, block)
-                    held = start if first else state[place]
-                    value = start + held * symbol_rows(unit, block, 0) + value
+                    value = start_of(unit, block) + state[place] * symbol_rows(unit, block, 0) + value
                     state[place] = value
                     now[0][place], now[1][place] = split(value)
 
-    def sweep(last):
-        order = ((0, 0), (0, 1), (1, 0), (1, 1))
-        for index, unit in enumerate(order):
-            if index + 1 < len(order):
-                issue(*order[index + 1])
-            elif not last:
-                issue(*order[0])
-            finish(*unit)
-            if last and unit[0] == 1:
-                done(unit[1])
+    def body(_, carry):
+        issue(0, 0)
+        finish(1, 1)
+        issue(0, 1)
+        finish(0, 0)
+        issue(1, 0)
+        finish(0, 1)
+        issue(1, 1)
+        finish(1, 0)
+        return carry
 
     for section in range(2):
         first_product(section)
         issue(1, section)
-    finish(1, 0, first=True)
-    issue(0, 0)
-    finish(1, 1, first=True)
-    lax.fori_loop(0, count - 2, lambda _, carry: (sweep(False), carry)[1], 0)
-    sweep(True)
+    finish(1, 0)
+    lax.fori_loop(0, count - 1, body, 0)
+    finish(1, 1)
 
 
 def product_kernel(*refs):
@@ -242,7 +238,7 @@
             out[target, :] = dot_split(split(value), pair(step))
 
 
-def unit_product(lhs, rhs, unit, sums):
+def unit_issue(lhs, rhs, unit, sums):
     depth = lhs[0].shape[1]
     tile = sums.shape[1]
     for first in range(0, depth, tile):
@@ -252,6 +248,10 @@
         pltpu.matmul_acc_lhs(sums, lhs[0][:, inner], load_staged_rhs=0)
         pltpu.matmul_acc_lhs(sums, lhs[1][:, inner])
         pltpu.matmul_acc_lhs(sums, lhs[0][:, inner], load_staged_rhs=1)
+
+
+def unit_product(lhs, rhs, unit, sums):
+    unit_issue(lhs, rhs, unit, sums)
     return pltpu.matmul_pop(sums)
 
 
@@ -290,49 +290,54 @@
         first = unit * half + block * BLOCK
         return product[first : first + BLOCK]
 
-    def to_panel(c, sums):
-        place = slice(c * 2 * lines, (c + 1) * 2 * lines)
-        unit = c * 2 * lines // half
-        value = unit_product((to_orders[0], to_orders[1]), (now[0].at[place], now[1].at[place]), unit, sums[unit])
-        value = split(value * factor)
-        cosine, sine = (
-            unit_product(
-                value,
-                tuple(inverse.at[part, :, unit * width : (unit + 1) * width] for part in range(2)),
-                unit,
-                sums[2 + unit],
-            )
-            for unit in range(2)
-        )
-        real = cosine[:rows] - sine[rows:]
-        imag = cosine[rows:] + sine[:rows]
-        for part, value in enumerate((real, imag)):
-            for first in range(0, yord, lines):
-                count = min(lines, yord - first)
-                result[c, first : first + count, part, :] = value[:count, :order]
-        pltpu.make_async_copy(result.at[c], out.at[c], ready.at[c]).start()
-
-    early = columns % 4 == 0 and half + 4 * rows <= SUM_ROWS
-
     def run(*sums):
-        blocks = 2 * (half // BLOCK)
-
-        def done(section):
-            if early:
-                quarter = columns // 4
-                for c in range(quarter):
-                    for unit in range(2):
-                        to_panel((2 * unit + section) * quarter + c, sums[blocks:])
-
-        sweeps(2**NS_ITERS - 1, half, start_of, first_of, symbol, steps, state, now, other, sums[:blocks], done)
-
-    sum_types = [pltpu.ACC(i % 2)((2 * rows, width), jnp.float32) for i in range(4)]
-    block_types = [pltpu.ACC(unit)((BLOCK, width), jnp.float32) for unit in range(2) for _ in range(half // BLOCK)]
-    pl.run_scoped(run, *block_types, *(sum_types if early else []))
-    if not early:
-        pl.run_scoped(lambda *sums: [to_panel(c, sums) for c in range(columns)] and None, *sum_types)
+        sweeps(2**NS_ITERS - 1, half, start_of, first_of, symbol, steps, state, now, other, sums)
+
+    pl.run_scoped(run, *[pltpu.ACC(unit)((BLOCK, width), jnp.float32) for unit in range(2) for _ in range(half // BLOCK)])
+
+    def copy_out(c):
+        return pltpu.make_async_copy(result.at[c], out.at[c], ready.at[c])
+
+    unit_of = [c * 2 * lines // half if columns > 1 else 0 for c in range(columns)]
+    order_of = sorted(range(columns), key=lambda c: (c % max(columns // 2, 1), c))
+    buffers = min(2, columns)
+
+    def all_columns(*sums):
+        in_orders, in_panel = sums[:columns], sums[columns:]
+
+        def transform(index):
+            c = order_of[index]
+            value = split(pltpu.matmul_pop(in_orders[c]) * factor)
+            for side in range(2):
+                table_of = tuple(inverse.at[part, :, side * width : (side + 1) * width] for part in range(2))
+                unit_issue(value, table_of, side, in_panel[2 * (index % buffers) + side])
+
+        def leave(index):
+            c = order_of[index]
+            cosine, sine = (pltpu.matmul_pop(in_panel[2 * (index % buffers) + side]) for side in range(2))
+            real = cosine[:rows] - sine[rows:]
+            imag = cosine[rows:] + sine[:rows]
+            for part, value in enumerate((real, imag)):
+                for first in range(0, yord, lines):
+                    count = min(lines, yord - first)
+                    result[c, first : first + count, part, :] = value[:count, :order]
+            copy_out(c).start()
+
+        for c in order_of:
+            place = slice(c * 2 * lines, (c + 1) * 2 * lines)
+            unit_issue((to_orders[0], to_orders[1]), (now[0].at[place], now[1].at[place]), unit_of[c], in_orders[c])
+        for index in range(columns):
+            transform(index)
+            if index + 1 >= buffers:
+                leave(index + 1 - buffers)
+        for index in range(columns + 1 - buffers, columns):
+            leave(index)
+
+    column_sums = [pltpu.ACC(unit)((2 * rows, width), jnp.float32) for unit in unit_of]
+    panel_sums = [pltpu.ACC(i % 2)((2 * rows, width), jnp.float32) for i in range(2 * buffers)]
+    pl.run_scoped(all_columns, *column_sums, *panel_sums)
     for c in range(columns):
-        pltpu.make_async_copy(result.at[c], out.at[c], ready.at[c]).wait()
+        copy_out(c).wait()
 
 
 SMEM = pl.BlockSpec(memory_space=pltpu.SMEM)

time: 28.4 us -> 27.6 us (0.972)
  Pallas kernels: 16.4 us -> 15.6 us
    pallas_call x1, Pallas kernels: 10.2 us -> 9.38 us  [local(): pl.pallas_call(functools.partial(apply_kernel, owners), out_shape=jax.Sha...]
where the time goes in v4:
time: 27.6 us; the launch traced here: 27.4 us
  Pallas kernels  15.6 us (57%)
  starting transfers between devices  8.09 us (29%)
  waiting for transfers between devices  3.62 us (13%)
    pallas_call x1, Pallas kernels, local(): pl.pallas_call(functools.partial(apply_kernel, owners), out_shape=jax.Sha...  9.38 us
    ppermute x5, starting transfers between devices, exchange(): lax.ppermute(block, 'long', [(i, i ^ distance) for i in range(devices)])  8.09 us
    ppermute x5, waiting for transfers between devices, exchange(): lax.ppermute(block, 'long', [(i, i ^ distance) for i in range(devices)])  3.62 us
    pallas_call x2, Pallas kernels, local(): pl.pallas_call(spread_kernel, grid=(1,), out_shape=jax.ShapeDtypeStruct((...  3.59 us
    pallas_call x1, Pallas kernels, local(): pl.pallas_call(coefficient_kernel, out_shape=jax.ShapeDtypeStruct((own, 2...  1.98 us
    pallas_call x1, Pallas kernels, local(): pl.pallas_call(product_kernel, out_shape=[jax.ShapeDtypeStruct((total, wi...  0.6 us
  transfers between devices with their start and end apart: 5, of which 4 were waited for; matrix products, arithmetic and copies ran while one was open for 0% of the time, Pallas kernels for 15%

profile of v4, /device:TPU:0, one launch (start us, length us, event | category | flops | bytes accessed | tf_op | source)
XLA Modules:
  0.0 27.4 jit_solution(4814007103490939152)
XLA Ops:
  0.0 0.0 copy-start.7
  0.0 0.0 copy-start.9
  0.0 0.0 copy-start.6
  0.0 2.0 %coefficient.1.refs_0_ = f32[8,512]{1,0:T(8,128)} custom-call(f32[4]{0:T(128)} %mats.3, s32[8,2048]{1,0:T(8,128)} %pixels.1, bf16[2,128,512]{2,1,0:T(8,128)(2,1)} %constant.18.clone.inner, f32[16,512]{1,0:T(8,128)} %constant.19.clone.outer), custom_call_target="tpu_custom_call" | custom-call | flops 3000000000 | bytes 4194304 | tf_op jit(solution)/shard_map/coefficient/pallas_call | solution.py:381
  2.0 4.1 %collective-permute-start = (f32[8,512]{1,0:T(8,128)}, f32[8,512]{1,0:T(8,128)S(1)}, u32[]{:S(2)}, u32[]{:S(2)}) collective-permute-start(f32[8,512]{1,0:T(8,128)} %coefficient.1.refs_0_), channel_id=1, source_target_pairs={{0,8},{1,9},{2,10},{3,11},{4,12},{5,13},{6,14},{7,15},{8,0},{9,1},... | collective-permute-start | bytes 49160 | tf_op jit(solution)/shard_map/ppermute | solution.py:395
  6.1 0.0 copy-done.7
  6.1 0.0 copy-done.9
  6.1 0.0 copy-done.6
  6.1 1.8 %spread.2.refs_0_ = f32[512,256]{1,0:T(8,128)S(1)} custom-call(f32[4,201,2,201]{3,2,1,0:T(2,128)S(1)} %bitcast.2, bf16[2,256,512]{2,1,0:T(8,128)(2,1)S(1)} %copy-done.7, bf16[2,256,256]{2,1,0:T(8,128)(2,1)S(1)} %copy-done.9), custom_call_target="tpu_custom_call" | custom-call | flops 1000000000 | bytes 2097152 | tf_op jit(solution)/shard_map/spread/pallas_call | solution.py:406
  7.9 0.1 collective-permute-done.refs_1_
  8.0 0.0 copy-done.4
  8.0 2.0 %collective-permute-start.1 = (f32[16,512]{1,0:T(8,128)S(1)}, f32[16,512]{1,0:T(8,128)S(1)}, u32[]{:S(2)}, u32[]{:S(2)}) collective-permute-start(f32[16,512]{1,0:T(8,128)S(1)} %join.2), channel_id=1, source_target_pairs={{0,4},{1,5},{2,6},{3,7},{4,0},{5,1},{6,2},{7,3},{8,12},{9,13},{10,... | collective-permute-start | bytes 98312 | tf_op jit(solution)/shard_map/ppermute | solution.py:395
  10.0 1.8 %spread.3.refs_1_ = f32[512,256]{1,0:T(8,128)S(1)} custom-call(f32[4,201,2,201]{3,2,1,0:T(2,128)S(1)} %bitcast.3, bf16[2,256,512]{2,1,0:T(8,128)(2,1)S(1)} %copy-done.7, bf16[2,256,256]{2,1,0:T(8,128)(2,1)S(1)} %copy-done.9), custom_call_target="tpu_custom_call" | custom-call | flops 1000000000 | bytes 2097152 | tf_op jit(solution)/shard_map/spread/pallas_call | solution.py:406
  11.8 0.2 collective-permute-done.1.refs_2_
  12.0 0.0 copy-start.1
  12.0 0.0 copy-start.2
  12.0 0.0 copy-start.3
  12.0 0.0 copy-start.5
  12.0 0.1 collective-permute-start.3
  12.1 2.0 %collective-permute-start.2 = (f32[32,512]{1,0:T(8,128)S(1)}, f32[32,512]{1,0:T(8,128)S(1)}, u32[]{:S(2)}, u32[]{:S(2)}) collective-permute-start(f32[32,512]{1,0:T(8,128)S(1)} %join.3.refs_0_), channel_id=1, source_target_pairs={{0,2},{1,3},{2,0},{3,1},{4,6},{5,7},{6,4},{7,5},{8,10},{9,11},{10,... | collective-permute-start | bytes 196616 | tf_op jit(solution)/shard_map/ppermute | solution.py:395
  14.1 0.0 copy-done.8
  14.1 0.6 %product.1 = (f32[1024,256]{1,0:T(8,128)S(1)}, f32[1024,256]{1,0:T(8,128)S(1)}) custom-call(f32[512,256]{1,0:T(8,128)S(1)} %spread.2.refs_0_, f32[512,256]{1,0:T(8,128)S(1)} %spread.3.refs_1_, bf16[2,256,256]{2,1,0:T(8,128)(2,1)S(1)} %copy-done.8), custom_call_target="tpu_custom_call" | custom-call | flops 1000000000 | bytes 2097152 | tf_op jit(solution)/shard_map/product/pallas_call | solution.py:420
  14.7 2.1 %collective-permute-done.2.refs_2_ = f32[32,512]{1,0:T(8,128)S(1)} collective-permute-done((f32[32,512]{1,0:T(8,128)S(1)}, f32[32,512]{1,0:T(8,128)S(1)}, u32[]{:S(2)}, u32[]{:S(2)}) %collective-permute-start.2) | collective-permute-done | bytes 65568 | tf_op jit(solution)/shard_map/ppermute | solution.py:395
  16.8 0.0 collective-permute-start.4
  16.8 0.0 collective-permute-done.3.refs_1_
  16.8 1.2 %collective-permute-done.4.refs_3_ = f32[32,512]{1,0:T(8,128)S(1)} collective-permute-done((f32[32,512]{1,0:T(8,128)S(1)}, f32[32,512]{1,0:T(8,128)S(1)}, u32[]{:S(2)}, u32[]{:S(2)}) %collective-permute-start.4) | collective-permute-done | bytes 65568 | tf_op jit(solution)/shard_map/ppermute | solution.py:395
  18.0 0.0 copy-done
  18.0 0.0 copy-done.1
  18.0 0.0 copy-done.2
  18.0 0.0 copy-done.3
  18.0 0.0 copy-done.5
  18.1 9.4 %apply.1 = f32[4,201,2,201]{3,2,1,0:T(2,128)} custom-call(f32[4]{0:T(128)S(1)} %copy-done.5, f32[1024,256]{1,0:T(8,128)S(1)} %get-tuple-element.20.start, f32[1024,256]{1,0:T(8,128)S(1)} %get-tuple-element.21.product, f32[32,512]{1,0:T(8,128)S(1)} %join.3.refs_0_, f32[32,512]{1,0:T(8,128)S(1)} %collective-permute-done.3.refs_1_, ...), custom_call_target="tpu_custom_call" | custom-call | flops 1000000000 | bytes 4194304 | tf_op jit(solution)/shard_map/apply/pallas_call | solution.py:439
  (5 shorter events, 0.0 us)
Async XLA Ops:
  0.0 6.1 %copy-start.7 = (bf16[2,256,512]{2,1,0:T(8,128)(2,1)S(1)}, bf16[2,256,512]{2,1,0:T(8,128)(2,1)}, u32[]{:S(2)}) copy-start(bf16[2,256,512]{2,1,0:T(8,128)(2,1)} %constant.20.clone.forward) | copy-start | bytes 1572868
  0.0 6.1 %copy-start.9 = (bf16[2,256,256]{2,1,0:T(8,128)(2,1)S(1)}, bf16[2,256,256]{2,1,0:T(8,128)(2,1)}, u32[]{:S(2)}) copy-start(bf16[2,256,256]{2,1,0:T(8,128)(2,1)} %constant.21.clone.to_lines) | copy-start | bytes 786436
  0.0 6.1 %copy-start.6 = (f32[4,2,201,201]{3,1,2,0:T(2,128)S(1)}, f32[4,2,201,201]{3,1,2,0:T(2,128)}, u32[]{:S(2)}) copy-start(f32[4,2,201,201]{3,1,2,0:T(2,128)} %param.14) | copy-start | bytes 3878500
  2.0 6.0 %collective-permute-start = (f32[8,512]{1,0:T(8,128)}, f32[8,512]{1,0:T(8,128)S(1)}, u32[]{:S(2)}, u32[]{:S(2)}) collective-permute-start(f32[8,512]{1,0:T(8,128)} %coefficient.1.refs_0_), channel_id=1, source_target_pairs={{0,8},{1,9},{2,10},{3,11},{4,12},{5,13},{6,14},{7,15},{8,0},{9,1},... | collective-permute-start | bytes 49160 | tf_op jit(solution)/shard_map/ppermute | solution.py:395
  6.1 1.9 %copy-start.4 = (f32[8,512]{1,0:T(8,128)S(1)}, f32[8,512]{1,0:T(8,128)}, u32[]{:S(2)}) copy-start(f32[8,512]{1,0:T(8,128)} %coefficient.1.refs_0_) | copy-start | bytes 49156
  8.0 6.1 %copy-start.8 = (bf16[2,256,256]{2,1,0:T(8,128)(2,1)S(1)}, bf16[2,256,256]{2,1,0:T(8,128)(2,1)}, u32[]{:S(2)}) copy-start(bf16[2,256,256]{2,1,0:T(8,128)(2,1)} %constant.22.clone.refs_2_) | copy-start | bytes 786436
  8.0 4.0 %collective-permute-start.1 = (f32[16,512]{1,0:T(8,128)S(1)}, f32[16,512]{1,0:T(8,128)S(1)}, u32[]{:S(2)}, u32[]{:S(2)}) collective-permute-start(f32[16,512]{1,0:T(8,128)S(1)} %join.2), channel_id=1, source_target_pairs={{0,4},{1,5},{2,6},{3,7},{4,0},{5,1},{6,2},{7,3},{8,12},{9,13},{10,... | collective-permute-start | bytes 98312 | tf_op jit(solution)/shard_map/ppermute | solution.py:395
  12.0 6.1 %copy-start = (bf16[2,512,512]{2,1,0:T(8,128)(2,1)S(1)}, bf16[2,512,512]{2,1,0:T(8,128)(2,1)}, u32[]{:S(2)}) copy-start(bf16[2,512,512]{2,1,0:T(8,128)(2,1)} %constant.23.clone.refs_4_) | copy-start | bytes 3145732
  12.0 6.0 %copy-start.1 = (bf16[2,256,512]{2,1,0:T(8,128)(2,1)S(1)}, bf16[2,256,512]{2,1,0:T(8,128)(2,1)}, u32[]{:S(2)}) copy-start(bf16[2,256,512]{2,1,0:T(8,128)(2,1)} %constant.25.clone.refs_6_) | copy-start | bytes 1572868
  12.0 6.0 %copy-start.2 = (bf16[4,256,256]{2,1,0:T(8,128)(2,1)S(1)}, bf16[4,256,256]{2,1,0:T(8,128)(2,1)}, u32[]{:S(2)}) copy-start(bf16[4,256,256]{2,1,0:T(8,128)(2,1)} %constant.24.clone.refs_5_) | copy-start | bytes 1572868
  12.0 6.0 %copy-start.3 = (bf16[2,256,256]{2,1,0:T(8,128)(2,1)S(1)}, bf16[2,256,256]{2,1,0:T(8,128)(2,1)}, u32[]{:S(2)}) copy-start(bf16[2,256,256]{2,1,0:T(8,128)(2,1)} %constant.26.clone.refs_7_) | copy-start | bytes 786436
  12.0 6.0 %copy-start.5 = (f32[4]{0:T(128)S(1)}, f32[4]{0:T(128)}, u32[]{:S(2)}) copy-start(f32[4]{0:T(128)} %mats.3) | copy-start | bytes 52
  12.0 4.7 %collective-permute-start.3 = (f32[32,512]{1,0:T(8,128)S(1)}, f32[32,512]{1,0:T(8,128)S(1)}, u32[]{:S(2)}, u32[]{:S(2)}) collective-permute-start(f32[32,512]{1,0:T(8,128)S(1)} %join.3.refs_0_), channel_id=1, source_target_pairs={{0,1},{1,0},{2,3},{3,2},{4,5},{5,4},{6,7},{7,6},{8,9},{9,8},{10,11... | collective-permute-start | bytes 196616 | tf_op jit(solution)/shard_map/ppermute | solution.py:395
  12.1 4.7 %collective-permute-start.2 = (f32[32,512]{1,0:T(8,128)S(1)}, f32[32,512]{1,0:T(8,128)S(1)}, u32[]{:S(2)}, u32[]{:S(2)}) collective-permute-start(f32[32,512]{1,0:T(8,128)S(1)} %join.3.refs_0_), channel_id=1, source_target_pairs={{0,2},{1,3},{2,0},{3,1},{4,6},{5,7},{6,4},{7,5},{8,10},{9,11},{10,... | collective-permute-start | bytes 196616 | tf_op jit(solution)/shard_map/ppermute | solution.py:395
  16.8 1.3 %collective-permute-start.4 = (f32[32,512]{1,0:T(8,128)S(1)}, f32[32,512]{1,0:T(8,128)S(1)}, u32[]{:S(2)}, u32[]{:S(2)}) collective-permute-start(f32[32,512]{1,0:T(8,128)S(1)} %collective-permute-done.2.refs_2_), channel_id=1, source_target_pairs={{0,1},{1,0},{2,3},{3,2},{4,5},{5,4},{6,7},{7,6},{8,9},{9,8},{10,11... | collective-permute-start | bytes 196616 | tf_op jit(solution)/shard_map/ppermute | solution.py:395

commit v5 on v4

--- a/solution.py
+++ b/solution.py
@@ -226,6 +226,13 @@
     finish(1, 1)
 
 
+def symbol_kernel(mats, *refs):
+    pieces, table, out = refs[:-2], refs[-2], refs[-1]
+    factor = scale_of([mats[i] for i in range(NMAT)])[0, 0]
+    values = jnp.concatenate([piece[...] for piece in pieces], 0)
+    out[...] = 0.5 - (0.5 * factor) * dot_split(split(values), pair(table))
+
+
 def product_kernel(*refs):
     sources, step, both, out = refs[:-3], refs[-3], refs[-2], refs[-1]
     rows = sources[0].shape[0]
@@ -255,32 +262,34 @@
     return pltpu.matmul_pop(sums)
 
 
-def apply_kernel(owners, mats, start, product, *refs):
+def apply_kernel(owners, mats, start, product, early, last, *refs):
     me = lax.axis_index("long")
-    pieces, refs = refs[: len(owners)], refs[len(owners) :]
-    table, steps, inverse, to_orders, out, coefficients, symbol, state, result, ready, *splits = refs
+    table, steps, inverse, to_orders, out, symbol, state, result, ready, *splits = refs
     now, other = splits[:2], splits[2:]
     columns, yord, _, order = out.shape
-    lines = coefficients.shape[0]
+    lines = symbol.shape[0]
     width = state.shape[1]
     rows = to_orders.shape[1] // 2
     half = state.shape[0] // 2
     factor = scale_of([mats[i] for i in range(NMAT)])[0, 0]
 
-    for piece, ids in zip(pieces, owners):
-        own = piece.shape[0] // len(ids)
-        for index, distance in enumerate(ids):
-            place = pl.multiple_of((me ^ distance) * own, own)
-            coefficients[pl.ds(place, own), :] = piece[index * own : (index + 1) * own]
-    values = split(coefficients[...])
-
-    def all_symbols(*sums):
+    def place_of(distance, own):
+        return pl.ds(pl.multiple_of((me ^ distance) * own, own), own)
+
+    own = last.shape[0] // len(owners[-1])
+    values = split(last[...])
+
+    def last_symbols(*sums):
         for unit in range(2):
             columns_of = slice(unit * width, (unit + 1) * width)
             value = unit_product(values, (table.at[0, :, columns_of], table.at[1, :, columns_of]), unit, sums[unit])
-            symbol[:, columns_of] = 0.5 - (0.5 * factor) * value
-
-    pl.run_scoped(all_symbols, *[pltpu.ACC(unit)((lines, width), jnp.float32) for unit in range(2)])
+            value = 0.5 - (0.5 * factor) * value
+            for index, distance in enumerate(owners[-1]):
+                symbol[place_of(distance, own), columns_of] = value[index * own : (index + 1) * own]
+
+    for index, distance in enumerate(d for ids in owners[:-1] for d in ids):
+        symbol[place_of(distance, own), :] = early[index * own : (index + 1) * own, :]
+    pl.run_scoped(last_symbols, *[pltpu.ACC(unit)((last.shape[0], width), jnp.float32) for unit in range(2)])
 
     def start_of(unit, block):
         first = unit * half + block * BLOCK
@@ -435,14 +444,24 @@
             owners.append(tuple(d ^ distance for d in ids))
         distance //= 2
 
+    table = symbol_table(order)
+    early = pl.pallas_call(
+        symbol_kernel,
+        out_shape=jax.ShapeDtypeStruct((sum(piece.shape[0] for piece in pieces[:-1]), 2 * width), jnp.float32),
+        in_specs=[SMEM] + [VMEM] * len(pieces),
+        out_specs=VMEM,
+        compiler_params=limit,
+        cost_estimate=pl.CostEstimate(flops=10**9, bytes_accessed=2**21, transcendentals=0),
+        name="symbol",
+    )(materials, *pieces[:-1], table)
+    early, last = lax.optimization_barrier((early, pieces[-1]))
     half = [pltpu.VMEM((total, width), jnp.bfloat16)]
     result = pl.pallas_call(
         functools.partial(apply_kernel, owners),
         out_shape=jax.ShapeDtypeStruct(by_order.shape, jnp.float32),
-        in_specs=[SMEM] + [VMEM] * (6 + len(pieces)),
+        in_specs=[SMEM] + [VMEM] * 8,
         out_specs=pl.BlockSpec(memory_space=pl.ANY),
         scratch_shapes=[
-            pltpu.VMEM((lines, 2 * width), jnp.float32),
             pltpu.VMEM((lines, 2 * width), jnp.float32),
             pltpu.VMEM((total, width), jnp.float32),
             pltpu.VMEM(by_order.shape, jnp.float32),
@@ -456,8 +475,9 @@
         materials,
         start,
         product,
-        *pieces,
-        symbol_table(order),
+        early,
+        last,
+        table,
         np.concatenate([step, back]),
         inverse,
         to_orders,

time: 27.6 us -> 27.5 us (level)
  waiting for transfers between devices: 3.62 us -> 2.66 us
  Pallas kernels: 15.6 us -> 16.4 us
    ppermute x5, waiting for transfers between devices: 3.62 us -> 2.66 us  [exchange(): lax.ppermute(block, 'long', [(i, i ^ distance) for i in range(devices)])]
    pallas_call x0 -> x1, Pallas kernels: none -> 0.93 us  [local(): pl.pallas_call(symbol_kernel, out_shape=jax.ShapeDtypeStruct((sum((piece....]
  transfers between devices with their start and end apart: 5 -> 5, of which waited for: 4 -> 4; matrix products, arithmetic and copies ran while one was open for 0% -> 0% of each run, Pallas kernels for 15% -> 19%
where the time goes in v5:
time: 27.5 us; the launch traced here: 27.3 us
  Pallas kernels  16.4 us (60%)
  starting transfers between devices  8.09 us (29%)
  waiting for transfers between devices  2.66 us (10%)
    pallas_call x1, Pallas kernels, local(): pl.pallas_call(functools.partial(apply_kernel, owners), out_shape=jax.Sha...  9.32 us
    ppermute x5, starting transfers between devices, exchange(): lax.ppermute(block, 'long', [(i, i ^ distance) for i in range(devices)])  8.09 us
    pallas_call x2, Pallas kernels, local(): pl.pallas_call(spread_kernel, grid=(1,), out_shape=jax.ShapeDtypeStruct((...  3.59 us
    ppermute x5, waiting for transfers between devices, exchange(): lax.ppermute(block, 'long', [(i, i ^ distance) for i in range(devices)])  2.66 us
    pallas_call x1, Pallas kernels, local(): pl.pallas_call(coefficient_kernel, out_shape=jax.ShapeDtypeStruct((own, 2...  1.98 us
    pallas_call x1, Pallas kernels, local(): pl.pallas_call(symbol_kernel, out_shape=jax.ShapeDtypeStruct((sum((piece....  0.93 us
    pallas_call x1, Pallas kernels, local(): pl.pallas_call(product_kernel, out_shape=[jax.ShapeDtypeStruct((total, wi...  0.6 us
  transfers between devices with their start and end apart: 5, of which 4 were waited for; matrix products, arithmetic and copies ran while one was open for 0% of the time, Pallas kernels for 19%

profile of v5, /device:TPU:0, one launch (start us, length us, event | category | flops | bytes accessed | tf_op | source)
XLA Modules:
  0.0 27.3 jit_solution(2095636363494133205)
XLA Ops:
  0.0 0.0 copy-start.7
  0.0 0.0 copy-start.9
  0.0 2.0 %coefficient.1.refs_0_ = f32[8,512]{1,0:T(8,128)} custom-call(f32[4]{0:T(128)} %mats.5, s32[8,2048]{1,0:T(8,128)} %pixels.1, bf16[2,128,512]{2,1,0:T(8,128)(2,1)} %constant.18.clone.inner, f32[16,512]{1,0:T(8,128)} %constant.19.clone.outer), custom_call_target="tpu_custom_call" | custom-call | flops 3000000000 | bytes 4194304 | tf_op jit(solution)/shard_map/coefficient/pallas_call | solution.py:390
  2.0 4.1 %collective-permute-start = (f32[8,512]{1,0:T(8,128)}, f32[8,512]{1,0:T(8,128)S(1)}, u32[]{:S(2)}, u32[]{:S(2)}) collective-permute-start(f32[8,512]{1,0:T(8,128)} %coefficient.1.refs_0_), channel_id=1, source_target_pairs={{0,8},{1,9},{2,10},{3,11},{4,12},{5,13},{6,14},{7,15},{8,0},{9,1},... | collective-permute-start | bytes 49160 | tf_op jit(solution)/shard_map/ppermute | solution.py:404
  6.1 0.0 copy-done.7
  6.1 0.0 copy-done.9
  6.1 0.0 copy-done.6
  6.1 0.0 copy-start.4
  6.1 1.8 %spread.2.refs_0_ = f32[512,256]{1,0:T(8,128)S(1)} custom-call(f32[4,201,2,201]{3,2,1,0:T(2,128)S(1)} %bitcast.2, bf16[2,256,512]{2,1,0:T(8,128)(2,1)S(1)} %copy-done.7, bf16[2,256,256]{2,1,0:T(8,128)(2,1)S(1)} %copy-done.9), custom_call_target="tpu_custom_call" | custom-call | flops 1000000000 | bytes 2097152 | tf_op jit(solution)/shard_map/spread/pallas_call | solution.py:415
  7.9 0.1 collective-permute-done.refs_1_
  8.0 0.0 copy-done.4
  8.0 0.0 copy-start.8
  8.0 2.0 %collective-permute-start.1 = (f32[16,512]{1,0:T(8,128)S(1)}, f32[16,512]{1,0:T(8,128)S(1)}, u32[]{:S(2)}, u32[]{:S(2)}) collective-permute-start(f32[16,512]{1,0:T(8,128)S(1)} %join.2), channel_id=1, source_target_pairs={{0,4},{1,5},{2,6},{3,7},{4,0},{5,1},{6,2},{7,3},{8,12},{9,13},{10,... | collective-permute-start | bytes 98312 | tf_op jit(solution)/shard_map/ppermute | solution.py:404
  10.0 1.8 %spread.3.refs_1_ = f32[512,256]{1,0:T(8,128)S(1)} custom-call(f32[4,201,2,201]{3,2,1,0:T(2,128)S(1)} %bitcast.3, bf16[2,256,512]{2,1,0:T(8,128)(2,1)S(1)} %copy-done.7, bf16[2,256,256]{2,1,0:T(8,128)(2,1)S(1)} %copy-done.9), custom_call_target="tpu_custom_call" | custom-call | flops 1000000000 | bytes 2097152 | tf_op jit(solution)/shard_map/spread/pallas_call | solution.py:415
  11.8 0.2 collective-permute-done.1.refs_2_
  12.0 0.0 copy-start.5
  12.0 0.1 collective-permute-start.3
  12.1 2.0 %collective-permute-start.2 = (f32[32,512]{1,0:T(8,128)S(1)}, f32[32,512]{1,0:T(8,128)S(1)}, u32[]{:S(2)}, u32[]{:S(2)}) collective-permute-start(f32[32,512]{1,0:T(8,128)S(1)} %join.3.refs_0_), channel_id=1, source_target_pairs={{0,2},{1,3},{2,0},{3,1},{4,6},{5,7},{6,4},{7,5},{8,10},{9,11},{10,... | collective-permute-start | bytes 196616 | tf_op jit(solution)/shard_map/ppermute | solution.py:404
  14.0 0.0 copy-done.8
  14.0 0.6 %product.1 = (f32[1024,256]{1,0:T(8,128)S(1)}, f32[1024,256]{1,0:T(8,128)S(1)}) custom-call(f32[512,256]{1,0:T(8,128)S(1)} %spread.2.refs_0_, f32[512,256]{1,0:T(8,128)S(1)} %spread.3.refs_1_, bf16[2,256,256]{2,1,0:T(8,128)(2,1)S(1)} %copy-done.8), custom_call_target="tpu_custom_call" | custom-call | flops 1000000000 | bytes 2097152 | tf_op jit(solution)/shard_map/product/pallas_call | solution.py:429
  14.7 2.1 %collective-permute-done.2.refs_2_ = f32[32,512]{1,0:T(8,128)S(1)} collective-permute-done((f32[32,512]{1,0:T(8,128)S(1)}, f32[32,512]{1,0:T(8,128)S(1)}, u32[]{:S(2)}, u32[]{:S(2)}) %collective-permute-start.2) | collective-permute-done | bytes 65568 | tf_op jit(solution)/shard_map/ppermute | solution.py:404
  16.7 0.0 copy-start.1
  16.7 0.0 collective-permute-start.4
  16.7 0.0 collective-permute-done.3.refs_1_
  16.8 0.0 copy-done
  16.8 0.0 copy-done.5
  16.8 0.9 %symbol.1.early = f32[96,512]{1,0:T(8,128)S(1)} custom-call(f32[4]{0:T(128)S(1)} %copy-done.5, f32[32,512]{1,0:T(8,128)S(1)} %join.3.refs_0_, f32[32,512]{1,0:T(8,128)S(1)} %collective-permute-done.3.refs_1_, f32[32,512]{1,0:T(8,128)S(1)} %collective-permute-done.2.refs_2_, bf16[2,512,512]{2,1,0:T(8,128)(2,1)S(1)} %copy-done), custom_call_target="tpu_custom_call" | custom-call | flops 1000000000 | bytes 2097152 | tf_op jit(solution)/shard_map/symbol/pallas_call | solution.py:448
  17.7 0.3 %collective-permute-done.4.last = f32[32,512]{1,0:T(8,128)S(1)} collective-permute-done((f32[32,512]{1,0:T(8,128)S(1)}, f32[32,512]{1,0:T(8,128)S(1)}, u32[]{:S(2)}, u32[]{:S(2)}) %collective-permute-start.4) | collective-permute-done | bytes 65568 | tf_op jit(solution)/shard_map/ppermute | solution.py:404
  18.0 0.0 copy-done.1
  18.0 0.0 copy-done.2
  18.0 0.0 copy-done.3
  18.0 9.3 %apply.1 = f32[4,201,2,201]{3,2,1,0:T(2,128)} custom-call(f32[4]{0:T(128)S(1)} %copy-done.5, f32[1024,256]{1,0:T(8,128)S(1)} %get-tuple-element.22.start, f32[1024,256]{1,0:T(8,128)S(1)} %get-tuple-element.23.product, f32[96,512]{1,0:T(8,128)S(1)} %symbol.1.early, f32[32,512]{1,0:T(8,128)S(1)} %collective-permute-done.4.last, ...), custom_call_target="tpu_custom_call" | custom-call | flops 1000000000 | bytes 4194304 | tf_op jit(solution)/shard_map/apply/pallas_call | solution.py:459
  (6 shorter events, 0.0 us)
Async XLA Ops:
  0.0 6.1 %copy-start.7 = (bf16[2,256,512]{2,1,0:T(8,128)(2,1)S(1)}, bf16[2,256,512]{2,1,0:T(8,128)(2,1)}, u32[]{:S(2)}) copy-start(bf16[2,256,512]{2,1,0:T(8,128)(2,1)} %constant.20.clone.forward) | copy-start | bytes 1572868
  0.0 6.1 %copy-start.9 = (bf16[2,256,256]{2,1,0:T(8,128)(2,1)S(1)}, bf16[2,256,256]{2,1,0:T(8,128)(2,1)}, u32[]{:S(2)}) copy-start(bf16[2,256,256]{2,1,0:T(8,128)(2,1)} %constant.21.clone.to_lines) | copy-start | bytes 786436
  0.0 6.1 %copy-start.6 = (f32[4,2,201,201]{3,1,2,0:T(2,128)S(1)}, f32[4,2,201,201]{3,1,2,0:T(2,128)}, u32[]{:S(2)}) copy-start(f32[4,2,201,201]{3,1,2,0:T(2,128)} %param.14) | copy-start | bytes 3878500
  2.0 6.0 %collective-permute-start = (f32[8,512]{1,0:T(8,128)}, f32[8,512]{1,0:T(8,128)S(1)}, u32[]{:S(2)}, u32[]{:S(2)}) collective-permute-start(f32[8,512]{1,0:T(8,128)} %coefficient.1.refs_0_), channel_id=1, source_target_pairs={{0,8},{1,9},{2,10},{3,11},{4,12},{5,13},{6,14},{7,15},{8,0},{9,1},... | collective-permute-start | bytes 49160 | tf_op jit(solution)/shard_map/ppermute | solution.py:404
  6.1 1.9 %copy-start.4 = (f32[8,512]{1,0:T(8,128)S(1)}, f32[8,512]{1,0:T(8,128)}, u32[]{:S(2)}) copy-start(f32[8,512]{1,0:T(8,128)} %coefficient.1.refs_0_) | copy-start | bytes 49156
  8.0 6.1 %copy-start.8 = (bf16[2,256,256]{2,1,0:T(8,128)(2,1)S(1)}, bf16[2,256,256]{2,1,0:T(8,128)(2,1)}, u32[]{:S(2)}) copy-start(bf16[2,256,256]{2,1,0:T(8,128)(2,1)} %constant.22.clone.refs_2_) | copy-start | bytes 786436
  8.0 4.0 %collective-permute-start.1 = (f32[16,512]{1,0:T(8,128)S(1)}, f32[16,512]{1,0:T(8,128)S(1)}, u32[]{:S(2)}, u32[]{:S(2)}) collective-permute-start(f32[16,512]{1,0:T(8,128)S(1)} %join.2), channel_id=1, source_target_pairs={{0,4},{1,5},{2,6},{3,7},{4,0},{5,1},{6,2},{7,3},{8,12},{9,13},{10,... | collective-permute-start | bytes 98312 | tf_op jit(solution)/shard_map/ppermute | solution.py:404
  12.0 4.8 %copy-start = (bf16[2,512,512]{2,1,0:T(8,128)(2,1)S(1)}, bf16[2,512,512]{2,1,0:T(8,128)(2,1)}, u32[]{:S(2)}) copy-start(bf16[2,512,512]{2,1,0:T(8,128)(2,1)} %constant.23.clone.refs_3_.refs_0_) | copy-start | bytes 3145732
  12.0 4.8 %copy-start.5 = (f32[4]{0:T(128)S(1)}, f32[4]{0:T(128)}, u32[]{:S(2)}) copy-start(f32[4]{0:T(128)} %mats.5) | copy-start | bytes 52
  12.0 4.8 %collective-permute-start.3 = (f32[32,512]{1,0:T(8,128)S(1)}, f32[32,512]{1,0:T(8,128)S(1)}, u32[]{:S(2)}, u32[]{:S(2)}) collective-permute-start(f32[32,512]{1,0:T(8,128)S(1)} %join.3.refs_0_), channel_id=1, source_target_pairs={{0,1},{1,0},{2,3},{3,2},{4,5},{5,4},{6,7},{7,6},{8,9},{9,8},{10,11... | collective-permute-start | bytes 196616 | tf_op jit(solution)/shard_map/ppermute | solution.py:404
  12.1 4.7 %collective-permute-start.2 = (f32[32,512]{1,0:T(8,128)S(1)}, f32[32,512]{1,0:T(8,128)S(1)}, u32[]{:S(2)}, u32[]{:S(2)}) collective-permute-start(f32[32,512]{1,0:T(8,128)S(1)} %join.3.refs_0_), channel_id=1, source_target_pairs={{0,2},{1,3},{2,0},{3,1},{4,6},{5,7},{6,4},{7,5},{8,10},{9,11},{10,... | collective-permute-start | bytes 196616 | tf_op jit(solution)/shard_map/ppermute | solution.py:404
  16.7 1.3 %copy-start.1 = (bf16[2,256,512]{2,1,0:T(8,128)(2,1)S(1)}, bf16[2,256,512]{2,1,0:T(8,128)(2,1)}, u32[]{:S(2)}) copy-start(bf16[2,256,512]{2,1,0:T(8,128)(2,1)} %constant.25.clone.refs_2_) | copy-start | bytes 1572868
  16.7 1.3 %copy-start.2 = (bf16[4,256,256]{2,1,0:T(8,128)(2,1)S(1)}, bf16[4,256,256]{2,1,0:T(8,128)(2,1)}, u32[]{:S(2)}) copy-start(bf16[4,256,256]{2,1,0:T(8,128)(2,1)} %constant.24.clone.refs_1_) | copy-start | bytes 1572868
  16.7 1.3 %copy-start.3 = (bf16[2,256,256]{2,1,0:T(8,128)(2,1)S(1)}, bf16[2,256,256]{2,1,0:T(8,128)(2,1)}, u32[]{:S(2)}) copy-start(bf16[2,256,256]{2,1,0:T(8,128)(2,1)} %constant.26.clone.refs_3_) | copy-start | bytes 786436
  16.7 1.3 %collective-permute-start.4 = (f32[32,512]{1,0:T(8,128)S(1)}, f32[32,512]{1,0:T(8,128)S(1)}, u32[]{:S(2)}, u32[]{:S(2)}) collective-permute-start(f32[32,512]{1,0:T(8,128)S(1)} %collective-permute-done.2.refs_2_), channel_id=1, source_target_pairs={{0,1},{1,0},{2,3},{3,2},{4,5},{5,4},{6,7},{7,6},{8,9},{9,8},{10,11... | collective-permute-start | bytes 196616 | tf_op jit(solution)/shard_map/ppermute | solution.py:404

commit v6 on v5

--- a/solution.py
+++ b/solution.py
@@ -435,8 +435,9 @@
                 cost_estimate=pl.CostEstimate(flops=10**9, bytes_accessed=2**21, transcendentals=0),
                 name="product",
             )(*starts, step)
-            start, product, other = lax.optimization_barrier((start, product, other))
-            beside = exchange(held, 1)
+            start, product, late = lax.optimization_barrier((start, product, held))
+            product, other = lax.optimization_barrier((product, other))
+            beside = exchange(late, 1)
             pieces = [held, beside, other, exchange(other, 1)]
             owners = [ids, tuple(d ^ 1 for d in ids), tuple(d ^ 2 for d in ids), tuple(d ^ 3 for d in ids)]
         else:

time: 27.5 us -> 27 us (0.982)
  waiting for transfers between devices: 2.66 us -> 2.24 us
    ppermute x5, waiting for transfers between devices: 2.66 us -> 2.24 us  [exchange(): lax.ppermute(block, 'long', [(i, i ^ distance) for i in range(devices)])]
where the time goes in v6:
time: 27 us; the launch traced here: 26.9 us
  Pallas kernels  16.4 us (61%)
  starting transfers between devices  8.09 us (30%)
  waiting for transfers between devices  2.24 us (8%)
    pallas_call x1, Pallas kernels, local(): pl.pallas_call(functools.partial(apply_kernel, owners), out_shape=jax.Sha...  9.32 us
    ppermute x5, starting transfers between devices, exchange(): lax.ppermute(block, 'long', [(i, i ^ distance) for i in range(devices)])  8.09 us
    pallas_call x2, Pallas kernels, local(): pl.pallas_call(spread_kernel, grid=(1,), out_shape=jax.ShapeDtypeStruct((...  3.59 us
    ppermute x5, waiting for transfers between devices, exchange(): lax.ppermute(block, 'long', [(i, i ^ distance) for i in range(devices)])  2.24 us
    pallas_call x1, Pallas kernels, local(): pl.pallas_call(coefficient_kernel, out_shape=jax.ShapeDtypeStruct((own, 2...  1.98 us
    pallas_call x1, Pallas kernels, local(): pl.pallas_call(symbol_kernel, out_shape=jax.ShapeDtypeStruct((sum((piece....  0.93 us
    pallas_call x1, Pallas kernels, local(): pl.pallas_call(product_kernel, out_shape=[jax.ShapeDtypeStruct((total, wi...  0.6 us
  transfers between devices with their start and end apart: 5, of which 4 were waited for; matrix products, arithmetic and copies ran while one was open for 0% of the time, Pallas kernels for 19%

profile of v6, /device:TPU:0, one launch (start us, length us, event | category | flops | bytes accessed | tf_op | source)
XLA Modules:
  0.0 26.9 jit_solution(4213677462487457861)
XLA Ops:
  0.0 0.0 copy-start.7
  0.0 0.0 copy-start.9
  0.0 2.0 %coefficient.1.refs_0_ = f32[8,512]{1,0:T(8,128)} custom-call(f32[4]{0:T(128)} %mats.5, s32[8,2048]{1,0:T(8,128)} %pixels.1, bf16[2,128,512]{2,1,0:T(8,128)(2,1)} %constant.18.clone.inner, f32[16,512]{1,0:T(8,128)} %constant.19.clone.outer), custom_call_target="tpu_custom_call" | custom-call | flops 3000000000 | bytes 4194304 | tf_op jit(solution)/shard_map/coefficient/pallas_call | solution.py:390
  2.0 4.1 %collective-permute-start = (f32[8,512]{1,0:T(8,128)}, f32[8,512]{1,0:T(8,128)S(1)}, u32[]{:S(2)}, u32[]{:S(2)}) collective-permute-start(f32[8,512]{1,0:T(8,128)} %coefficient.1.refs_0_), channel_id=1, source_target_pairs={{0,8},{1,9},{2,10},{3,11},{4,12},{5,13},{6,14},{7,15},{8,0},{9,1},... | collective-permute-start | bytes 49160 | tf_op jit(solution)/shard_map/ppermute | solution.py:404
  6.1 0.0 copy-done.7
  6.1 0.0 copy-done.9
  6.1 0.0 copy-done.6
  6.1 1.8 %spread.2.refs_0_ = f32[512,256]{1,0:T(8,128)S(1)} custom-call(f32[4,201,2,201]{3,2,1,0:T(2,128)S(1)} %bitcast.2, bf16[2,256,512]{2,1,0:T(8,128)(2,1)S(1)} %copy-done.7, bf16[2,256,256]{2,1,0:T(8,128)(2,1)S(1)} %copy-done.9), custom_call_target="tpu_custom_call" | custom-call | flops 1000000000 | bytes 2097152 | tf_op jit(solution)/shard_map/spread/pallas_call | solution.py:415
  7.9 0.1 collective-permute-done.refs_1_
  8.0 0.0 copy-done.4
  8.0 2.0 %collective-permute-start.1 = (f32[16,512]{1,0:T(8,128)S(1)}, f32[16,512]{1,0:T(8,128)S(1)}, u32[]{:S(2)}, u32[]{:S(2)}) collective-permute-start(f32[16,512]{1,0:T(8,128)S(1)} %join.2), channel_id=1, source_target_pairs={{0,4},{1,5},{2,6},{3,7},{4,0},{5,1},{6,2},{7,3},{8,12},{9,13},{10,... | collective-permute-start | bytes 98312 | tf_op jit(solution)/shard_map/ppermute | solution.py:404
  10.0 1.8 %spread.3.refs_1_ = f32[512,256]{1,0:T(8,128)S(1)} custom-call(f32[4,201,2,201]{3,2,1,0:T(2,128)S(1)} %bitcast.3, bf16[2,256,512]{2,1,0:T(8,128)(2,1)S(1)} %copy-done.7, bf16[2,256,256]{2,1,0:T(8,128)(2,1)S(1)} %copy-done.9), custom_call_target="tpu_custom_call" | custom-call | flops 1000000000 | bytes 2097152 | tf_op jit(solution)/shard_map/spread/pallas_call | solution.py:415
  11.8 0.2 collective-permute-done.1.refs_2_
  12.0 0.0 copy-start.5
  12.0 2.0 %collective-permute-start.2 = (f32[32,512]{1,0:T(8,128)S(1)}, f32[32,512]{1,0:T(8,128)S(1)}, u32[]{:S(2)}, u32[]{:S(2)}) collective-permute-start(f32[32,512]{1,0:T(8,128)S(1)} %join.3.refs_0_), channel_id=1, source_target_pairs={{0,2},{1,3},{2,0},{3,1},{4,6},{5,7},{6,4},{7,5},{8,10},{9,11},{10,... | collective-permute-start | bytes 196616 | tf_op jit(solution)/shard_map/ppermute | solution.py:404
  14.0 0.0 copy-done.8
  14.0 0.6 %product.1 = (f32[1024,256]{1,0:T(8,128)S(1)}, f32[1024,256]{1,0:T(8,128)S(1)}) custom-call(f32[512,256]{1,0:T(8,128)S(1)} %spread.2.refs_0_, f32[512,256]{1,0:T(8,128)S(1)} %spread.3.refs_1_, bf16[2,256,256]{2,1,0:T(8,128)(2,1)S(1)} %copy-done.8), custom_call_target="tpu_custom_call" | custom-call | flops 1000000000 | bytes 2097152 | tf_op jit(solution)/shard_map/product/pallas_call | solution.py:429
  14.6 0.0 copy-start.1
  14.6 0.0 copy-start.2
  14.6 0.0 copy-start.3
  14.6 0.1 collective-permute-start.3
  14.7 1.6 %collective-permute-done.2.refs_2_ = f32[32,512]{1,0:T(8,128)S(1)} collective-permute-done((f32[32,512]{1,0:T(8,128)S(1)}, f32[32,512]{1,0:T(8,128)S(1)}, u32[]{:S(2)}, u32[]{:S(2)}) %collective-permute-start.2) | collective-permute-done | bytes 65568 | tf_op jit(solution)/shard_map/ppermute | solution.py:404
  16.3 0.0 collective-permute-start.4
  16.3 0.0 collective-permute-done.3.refs_1_
  16.3 0.0 copy-done
  16.3 0.0 copy-done.5
  16.3 0.9 %symbol.1.early = f32[96,512]{1,0:T(8,128)S(1)} custom-call(f32[4]{0:T(128)S(1)} %copy-done.5, f32[32,512]{1,0:T(8,128)S(1)} %join.3.refs_0_, f32[32,512]{1,0:T(8,128)S(1)} %collective-permute-done.3.refs_1_, f32[32,512]{1,0:T(8,128)S(1)} %collective-permute-done.2.refs_2_, bf16[2,512,512]{2,1,0:T(8,128)(2,1)S(1)} %copy-done), custom_call_target="tpu_custom_call" | custom-call | flops 1000000000 | bytes 2097152 | tf_op jit(solution)/shard_map/symbol/pallas_call | solution.py:449
  17.3 0.3 %collective-permute-done.4.last = f32[32,512]{1,0:T(8,128)S(1)} collective-permute-done((f32[32,512]{1,0:T(8,128)S(1)}, f32[32,512]{1,0:T(8,128)S(1)}, u32[]{:S(2)}, u32[]{:S(2)}) %collective-permute-start.4) | collective-permute-done | bytes 65568 | tf_op jit(solution)/shard_map/ppermute | solution.py:404
  17.6 0.0 copy-done.1
  17.6 0.0 copy-done.2
  17.6 0.0 copy-done.3
  17.6 9.3 %apply.1 = f32[4,201,2,201]{3,2,1,0:T(2,128)} custom-call(f32[4]{0:T(128)S(1)} %copy-done.5, f32[1024,256]{1,0:T(8,128)S(1)} %get-tuple-element.24.start, f32[1024,256]{1,0:T(8,128)S(1)} %get-tuple-element.26.product, f32[96,512]{1,0:T(8,128)S(1)} %symbol.1.early, f32[32,512]{1,0:T(8,128)S(1)} %collective-permute-done.4.last, ...), custom_call_target="tpu_custom_call" | custom-call | flops 1000000000 | bytes 4194304 | tf_op jit(solution)/shard_map/apply/pallas_call | solution.py:460
  (6 shorter events, 0.0 us)
Async XLA Ops:
  0.0 6.1 %copy-start.7 = (bf16[2,256,512]{2,1,0:T(8,128)(2,1)S(1)}, bf16[2,256,512]{2,1,0:T(8,128)(2,1)}, u32[]{:S(2)}) copy-start(bf16[2,256,512]{2,1,0:T(8,128)(2,1)} %constant.20.clone.forward) | copy-start | bytes 1572868
  0.0 6.1 %copy-start.9 = (bf16[2,256,256]{2,1,0:T(8,128)(2,1)S(1)}, bf16[2,256,256]{2,1,0:T(8,128)(2,1)}, u32[]{:S(2)}) copy-start(bf16[2,256,256]{2,1,0:T(8,128)(2,1)} %constant.21.clone.to_lines) | copy-start | bytes 786436
  0.0 6.1 %copy-start.6 = (f32[4,2,201,201]{3,1,2,0:T(2,128)S(1)}, f32[4,2,201,201]{3,1,2,0:T(2,128)}, u32[]{:S(2)}) copy-start(f32[4,2,201,201]{3,1,2,0:T(2,128)} %param.14) | copy-start | bytes 3878500
  2.0 6.0 %collective-permute-start = (f32[8,512]{1,0:T(8,128)}, f32[8,512]{1,0:T(8,128)S(1)}, u32[]{:S(2)}, u32[]{:S(2)}) collective-permute-start(f32[8,512]{1,0:T(8,128)} %coefficient.1.refs_0_), channel_id=1, source_target_pairs={{0,8},{1,9},{2,10},{3,11},{4,12},{5,13},{6,14},{7,15},{8,0},{9,1},... | collective-permute-start | bytes 49160 | tf_op jit(solution)/shard_map/ppermute | solution.py:404
  6.1 1.9 %copy-start.4 = (f32[8,512]{1,0:T(8,128)S(1)}, f32[8,512]{1,0:T(8,128)}, u32[]{:S(2)}) copy-start(f32[8,512]{1,0:T(8,128)} %coefficient.1.refs_0_) | copy-start | bytes 49156
  8.0 6.0 %copy-start.8 = (bf16[2,256,256]{2,1,0:T(8,128)(2,1)S(1)}, bf16[2,256,256]{2,1,0:T(8,128)(2,1)}, u32[]{:S(2)}) copy-start(bf16[2,256,256]{2,1,0:T(8,128)(2,1)} %constant.22.clone.refs_2_) | copy-start | bytes 786436
  8.0 4.0 %collective-permute-start.1 = (f32[16,512]{1,0:T(8,128)S(1)}, f32[16,512]{1,0:T(8,128)S(1)}, u32[]{:S(2)}, u32[]{:S(2)}) collective-permute-start(f32[16,512]{1,0:T(8,128)S(1)} %join.2), channel_id=1, source_target_pairs={{0,4},{1,5},{2,6},{3,7},{4,0},{5,1},{6,2},{7,3},{8,12},{9,13},{10,... | collective-permute-start | bytes 98312 | tf_op jit(solution)/shard_map/ppermute | solution.py:404
  12.0 4.4 %copy-start = (bf16[2,512,512]{2,1,0:T(8,128)(2,1)S(1)}, bf16[2,512,512]{2,1,0:T(8,128)(2,1)}, u32[]{:S(2)}) copy-start(bf16[2,512,512]{2,1,0:T(8,128)(2,1)} %constant.23.clone.refs_3_.refs_0_) | copy-start | bytes 3145732
  12.0 4.4 %copy-start.5 = (f32[4]{0:T(128)S(1)}, f32[4]{0:T(128)}, u32[]{:S(2)}) copy-start(f32[4]{0:T(128)} %mats.5) | copy-start | bytes 52
  12.0 4.3 %collective-permute-start.2 = (f32[32,512]{1,0:T(8,128)S(1)}, f32[32,512]{1,0:T(8,128)S(1)}, u32[]{:S(2)}, u32[]{:S(2)}) collective-permute-start(f32[32,512]{1,0:T(8,128)S(1)} %join.3.refs_0_), channel_id=1, source_target_pairs={{0,2},{1,3},{2,0},{3,1},{4,6},{5,7},{6,4},{7,5},{8,10},{9,11},{10,... | collective-permute-start | bytes 196616 | tf_op jit(solution)/shard_map/ppermute | solution.py:404
  14.6 3.0 %copy-start.1 = (bf16[2,256,512]{2,1,0:T(8,128)(2,1)S(1)}, bf16[2,256,512]{2,1,0:T(8,128)(2,1)}, u32[]{:S(2)}) copy-start(bf16[2,256,512]{2,1,0:T(8,128)(2,1)} %constant.25.clone.refs_2_) | copy-start | bytes 1572868
  14.6 3.0 %copy-start.2 = (bf16[4,256,256]{2,1,0:T(8,128)(2,1)S(1)}, bf16[4,256,256]{2,1,0:T(8,128)(2,1)}, u32[]{:S(2)}) copy-start(bf16[4,256,256]{2,1,0:T(8,128)(2,1)} %constant.24.clone.refs_1_) | copy-start | bytes 1572868
  14.6 3.0 %copy-start.3 = (bf16[2,256,256]{2,1,0:T(8,128)(2,1)S(1)}, bf16[2,256,256]{2,1,0:T(8,128)(2,1)}, u32[]{:S(2)}) copy-start(bf16[2,256,256]{2,1,0:T(8,128)(2,1)} %constant.26.clone.refs_3_) | copy-start | bytes 786436
  14.6 1.7 %collective-permute-start.3 = (f32[32,512]{1,0:T(8,128)S(1)}, f32[32,512]{1,0:T(8,128)S(1)}, u32[]{:S(2)}, u32[]{:S(2)}) collective-permute-start(f32[32,512]{1,0:T(8,128)S(1)} %join.3.refs_0_), channel_id=1, source_target_pairs={{0,1},{1,0},{2,3},{3,2},{4,5},{5,4},{6,7},{7,6},{8,9},{9,8},{10,11... | collective-permute-start | bytes 196616 | tf_op jit(solution)/shard_map/ppermute | solution.py:404
  16.3 1.3 %collective-permute-start.4 = (f32[32,512]{1,0:T(8,128)S(1)}, f32[32,512]{1,0:T(8,128)S(1)}, u32[]{:S(2)}, u32[]{:S(2)}) collective-permute-start(f32[32,512]{1,0:T(8,128)S(1)} %collective-permute-done.2.refs_2_), channel_id=1, source_target_pairs={{0,1},{1,0},{2,3},{3,2},{4,5},{5,4},{6,7},{7,6},{8,9},{9,8},{10,11... | collective-permute-start | bytes 196616 | tf_op jit(solution)/shard_map/ppermute | solution.py:404
